TPU v7x, 128 devices: a whole 4x4x4 slice. The times are simulated.
128 devices in a mesh: exp: 32 (over z, x_lo, y), row: 4 (over x_hi, core).
Axes of the slice: x: 4 (x_hi: 2, x_lo: 2; x = x_hi * 2 + x_lo), y: 4, z: 4, core: 2. Of those that a mesh axis runs over, the one named last changes fastest.
Arguments:
- latent: bfloat16 [4, 1024, 1024], P(None, 'row', 'exp'), may hold values from -6 to 6
- row_taps: bfloat16 [16, 21], replicated, may hold values from -1.25 to 1.25
- column_taps: bfloat16 [16, 21], replicated, may hold values from -1.25 to 1.25
- coefficients: bfloat16 [32, 16, 1024, 1024], P('exp', None, 'row'), may hold values from -1.5 to 1.5
- observed: bfloat16 [32, 1024, 1024], P('exp', 'row'), may hold values from -6 to 6
- cell_of: int32 [32, 1], replicated, may hold values from 0 to 3
- valid_rows: int32 [32, 1024], P('exp', 'row'), may hold values 0 or 1
Outputs:
- gradient: float32 [4, 1024, 1024], P(None, 'row', 'exp')
- residuals: float32 [32, 1024, 1024], P('exp', 'row')
Inputs may be any that keep to these rules, and one draw needn't show every extreme that they name: `cell_of`: every sky cell is covered by at least one exposure.
All inputs are finite; a program needn't handle non-finite values. No bound on the sum of `valid_rows` on one device may be relied on, other than what follows from the above.
Results may differ from a plain program's by a relative error of at most 0.0023.
Values may be sent and summed in bfloat16 or wider, within the bound.
No kernel may reach another device: no remote copies, remote signals or barrier semaphores. Data moves between devices by JAX's collectives and lax.ppermute only.
A program may use at most 128 MiB of HBM per device.

v0:
```python
import jax
import jax.numpy as jnp
from jax import lax
from jax.sharding import PartitionSpec as P


def padded_2(cells, sides, width):
    for axis, dim in sides:
        count = lax.axis_size(axis)
        ends = count - 1
        head = lax.slice_in_dim(cells, 0, width, axis=dim)
        tail = lax.slice_in_dim(cells, cells.shape[dim] - width, cells.shape[dim], axis=dim)
        cells = jnp.concatenate(
            [
                lax.ppermute(tail, axis, [(i, (i + 1) % count) for i in range(ends)]),
                cells,
                lax.ppermute(head, axis, [((i + 1) % count, i) for i in range(ends)]),
            ],
            axis=dim,
        )
    return cells


def from_behind(block, axis, distance):
    devices = range(lax.axis_size(axis))
    route = [(i - distance, i) for i in devices if i - distance in devices]
    return lax.ppermute(block, axis, route)


def bands(kernel_taps, adjoint):
    tap_count = kernel_taps.shape[1]
    halfwidth = tap_count // 2
    inputs_at = lax.broadcasted_iota(jnp.int32, (384, 128), 0)
    outputs_at = lax.broadcasted_iota(jnp.int32, (384, 128), 1)
    if adjoint:
        offset = outputs_at - inputs_at + 128 + halfwidth
    else:
        offset = inputs_at - 128 - outputs_at + halfwidth
    onehot = (offset[:, :, None] == jnp.arange(tap_count)[None, None, :]).astype(jnp.float32)
    return jnp.einsum("kt,pqt->kpq", kernel_taps.astype(jnp.float32), onehot).astype(jnp.bfloat16)


def column_matrix(kernel_taps, strip_rows):
    tap_count = kernel_taps.shape[1]
    halfwidth = tap_count // 2
    outputs_at = lax.broadcasted_iota(jnp.int32, (strip_rows, strip_rows + 2 * halfwidth), 0)
    inputs_at = lax.broadcasted_iota(jnp.int32, (strip_rows, strip_rows + 2 * halfwidth), 1)
    offset = inputs_at - outputs_at
    onehot = (offset[:, :, None] == jnp.arange(tap_count)[None, None, :]).astype(jnp.float32)
    return jnp.einsum("kt,yit->kyi", kernel_taps.astype(jnp.float32), onehot).astype(jnp.bfloat16)


def stacked_blocks(source):
    length = source.shape[-1]
    nblocks = length // 128
    padding = [(0, 0)] * (source.ndim - 1) + [(128, 128)]
    padded = jnp.pad(source, padding)
    blocked = padded.reshape(source.shape[:-1] + (nblocks + 2, 128))
    return jnp.concatenate(
        [blocked[..., :-2, :], blocked[..., 1:-1, :], blocked[..., 2:, :]], axis=-1
    )


def body(latent, row_taps, column_taps, coefficients, observed, cell_of, valid_rows):
    tap_count = row_taps.shape[1]
    halfwidth = tap_count // 2
    kernel_count = row_taps.shape[0]
    strip_rows = observed.shape[1]
    cell_width = observed.shape[2]
    ncells = latent.shape[0]
    position = lax.axis_index("exp")
    cell_list = cell_of[:, 0]
    own_cell = lax.dynamic_index_in_dim(cell_list, position, 0, keepdims=False)
    all_cells = lax.all_gather(latent, "exp", axis=2, tiled=True)
    cell_strip = lax.dynamic_index_in_dim(all_cells, own_cell, 0, keepdims=False)
    extended = padded_2(cell_strip, (("row", 0),), halfwidth)
    rowblur = jnp.einsum(
        "rbp,kpq->krbq",
        stacked_blocks(extended),
        bands(row_taps, False),
        preferred_element_type=jnp.float32,
    )
    rowblur = rowblur.reshape(kernel_count, strip_rows + 2 * halfwidth, cell_width).astype(
        jnp.bfloat16
    )
    matrix = column_matrix(column_taps, strip_rows)
    vertical = jnp.einsum("kyi,kix->kyx", matrix, rowblur, preferred_element_type=jnp.float32)
    coeffs = coefficients[0].astype(jnp.float32)
    predicted = jnp.sum(coeffs * vertical, axis=0)
    row_mask = valid_rows[0].astype(jnp.float32)[:, None]
    residual = row_mask * (predicted - observed[0].astype(jnp.float32))
    weighted = (coeffs * residual[None]).astype(jnp.bfloat16)
    colback_ext = jnp.einsum("kyi,kyx->kix", matrix, weighted, preferred_element_type=jnp.float32)
    upper_rim = colback_ext[:, :halfwidth]
    lower_rim = colback_ext[:, strip_rows + halfwidth :]
    from_below = from_behind(upper_rim.astype(jnp.bfloat16), "row", -1).astype(upper_rim.dtype)
    from_above = from_behind(lower_rim.astype(jnp.bfloat16), "row", 1).astype(lower_rim.dtype)
    middle = colback_ext[:, halfwidth : strip_rows + halfwidth]
    middle = middle.at[:, :halfwidth].add(from_above)
    middle = middle.at[:, strip_rows - halfwidth :].add(from_below)
    colback = middle.astype(jnp.bfloat16)
    own_term = jnp.einsum(
        "krbp,kpq->rbq",
        stacked_blocks(colback),
        bands(row_taps, True),
        preferred_element_type=jnp.float32,
    ).reshape(strip_rows, cell_width)
    selector = (jnp.arange(ncells) == own_cell).astype(jnp.float32)
    gradient = lax.psum_scatter(
        selector[:, None, None] * own_term[None], "exp", scatter_dimension=2, tiled=True
    )
    return (gradient, residual[None])


def solution(mesh):
    placed = (
        P(None, "row", "exp"),
        P(),
        P(),
        P("exp", None, "row", None),
        P("exp", "row", None),
        P(),
        P("exp", "row"),
    )
    return jax.shard_map(
        body,
        mesh=mesh,
        in_specs=placed,
        out_specs=(P(None, "row", "exp"), P("exp", "row", None)),
        check_vma=False,
    )
```

profile of v0, /device:TPU:4, one launch (start us, length us, event | category | flops | bytes accessed | tf_op | source)
XLA Modules:
  0.0 556.6 jit_solution(14296747167301705185)
XLA Ops:
  7.2 1.5 copy.41
  8.8 0.0 reduce-scatter.2.cloned.1.call-start
  8.8 1.2 constant_dynamic-slice_fusion.1
  11.7 0.1 subtract_add_fusion.1
  11.9 2.3 fusion.28
  14.2 2.2 convert_bitcast_fusion.1
  16.4 148.6 %all-gather.2.cloned.1.call-done = bf16[4,256,1024]{1,0,2:T(4,128)(2,1)} async-done(((bf16[4,256,32]{1,0,2:T(4,128)(2,1)}), bf16[4,256,1024]{1,0,2:T(4,128)(2,1)}) %all-gather.2.cloned.1.call-update) | async-done | bytes 2097168 | tf_op jit(solution)/shard_map/all_gather | solution.py:74
  165.0 2.7 constant_dynamic-slice_fusion
  167.7 2.3 copy.62
  170.0 0.8 slice_bitcast_fusion.1
  170.7 1.9 collective-permute-start
  172.7 5.3 collective-permute-start.1
  178.0 0.7 subtract_add_fusion
  178.7 0.7 collective-permute-done.1
  179.4 2.0 fusion.36
  181.4 1.5 reshape.134
  183.0 0.3 fusion.44
  183.3 0.1 copy.63
  183.4 0.1 copy.64
  183.5 0.1 copy.65
  183.5 0.8 copy-done.3
  184.4 7.2 %convert_bitcast_fusion = bf16[16,276,8,128]{3,1,2,0:T(8,128)(2,1)} fusion(bf16[276,8,128]{2,0,1:T(8,128)(2,1)S(1)} %copy.65, bf16[276,8,128]{2,0,1:T(8,128)(2,1)S(1)} %copy.64, bf16[276,8,128]{2,0,1:T(8,128)(2,1)S(1)} %copy.63, bf16[16,384,128,1]{2,0,1,3:T(8,128)(2,1)S(1)} %copy-done.3), kind=kOutput, calls=%fused_computation.10 | convolution fusion | flops 3482492928 | bytes 12312576 | tf_op jit(solution)/shard_map/rbp,kpq->krbq/dot_general | solution.py:77
  191.6 8.3 %copy.60 = bf16[16,276,8,128]{3,2,1,0:T(8,128)(2,1)} copy(bf16[16,276,8,128]{3,1,2,0:T(8,128)(2,1)} %convert_bitcast_fusion) | data formatting | bytes 18087936 | tf_op jit(solution)/shard_map/convert_element_type | solution.py:83
  199.9 14.0 %reshape.143 = bf16[16,276,1024]{2,1,0:T(8,128)(2,1)} reshape(bf16[16,276,8,128]{3,2,1,0:T(8,128)(2,1)} %copy.60) | data formatting | bytes 18087936 | tf_op jit(solution)/shard_map/convert_element_type | solution.py:83
  213.8 13.0 %fusion.6 = f32[256,1024]{1,0:T(8,128)S(1)} fusion(bf16[16,276,1024]{2,1,0:T(8,128)(2,1)} %reshape.143, bf16[1,16,256,1024]{3,2,1,0:T(8,128)(2,1)} %param.14, bf16[16,256,276]{1,0,2:T(8,128)(2,1)S(1)} %convert_bitcast_fusion.1), kind=kOutput, calls=%fused_computation.8 | convolution fusion | flops 2327576576 | bytes 20742144 | tf_op jit(solution)/shard_map/kyi,kix->kyx/dot_general | solution.py:87
  226.8 0.2 fusion.31
  227.0 17.7 %fusion.45 = (bf16[16,276,1024]{2,1,0:T(8,128)(2,1)}, f32[16,276,1024]{2,1,0:T(8,128)}) fusion(bf16[1,16,256,1024]{3,2,1,0:T(8,128)(2,1)} %param.14, f32[256,1024]{1,0:T(8,128)S(1)} %bitcast.54, bf16[16,256,276]{1,0,2:T(8,128)(2,1)S(1)} %convert_bitcast_fusion.1), kind=kOutput, calls=%fused_computation.67 | convolution fusion | flops 2332360704 | bytes 38830080 | tf_op jit(solution)/shard_map/kyi,kyx->kix/dot_general | solution.py:93
  244.7 2.4 fusion.43
  247.1 1.9 collective-permute-start.2
  249.0 1.1 fusion.29
  250.1 5.2 collective-permute-start.3
  255.3 0.5 compare_convert_fusion
  255.9 1.3 copy.55
  257.1 12.6 %slice.110 = f32[16,256,1024]{2,1,0:T(8,128)} slice(f32[16,276,1024]{2,1,0:T(8,128)} %get-tuple-element.37), slice={[0:16], [10:266], [0:1024]} | slice | bytes 33554432 | tf_op jit(solution)/shard_map/slice | solution.py:98
  269.7 1.7 slice_add_fusion.1
  271.4 5.8 %scatter-add.6 = f32[16,256,1024]{2,1,0:T(8,128)} dynamic-update-slice(f32[16,256,1024]{2,1,0:T(8,128)} %slice.110, f32[16,10,1024]{2,1,0:T(8,128)S(1)} %slice_add_fusion.1, s32[]{:T(128)} %constant.75.clone.1, s32[]{:T(128)} %constant.75.clone.1, s32[]{:T(128)} %constant.75.clone.1) | dynamic-update-slice | bytes 1310724 | tf_op jit(solution)/shard_map/scatter-add | solution.py:99
  277.3 1.5 slice_add_fusion
  278.8 5.1 scatter-add.9
  283.9 9.1 %convert_element_type.94 = bf16[16,256,1024]{2,1,0:T(8,128)(2,1)} convert(f32[16,256,1024]{2,1,0:T(8,128)} %scatter-add.9) | non-fusion elementwise | flops 4194304 | bytes 25165824 | tf_op jit(solution)/shard_map/convert_element_type | solution.py:101
  293.0 12.3 %copy.69 = bf16[16,256,1024]{1,2,0:T(8,128)(2,1)} copy(bf16[16,256,1024]{2,1,0:T(8,128)(2,1)} %convert_element_type.94) | data formatting | bytes 16777216
  305.3 8.4 %pad.13.clone = bf16[16,256,1280]{1,2,0:T(8,128)(2,1)} pad(bf16[16,256,1024]{1,2,0:T(8,128)(2,1)} %copy.69, bf16[]{:T(256)} %constant.80.clone.1), padding=0_0x0_0x128_128 | pad | bytes 18874370 | tf_op jit(solution)/shard_map/jit(_pad)/pad | solution.py:57
  313.7 16.7 %fusion.42 = (bf16[16,256,8,128]{1,3,2,0:T(8,128)(2,1)}, bf16[16,256,8,128]{1,3,2,0:T(8,128)(2,1)}, bf16[16,256,8,128]{1,3,2,0:T(8,128)(2,1)}) fusion(bf16[16,256,10,128]{1,3,2,0:T(8,128)(2,1)} %bitcast.53), kind=kLoop, calls=%fused_computation.64 | loop fusion | bytes 50331648 | tf_op jit(solution)/shard_map/slice | solution.py:60
  330.4 11.4 %copy.66 = bf16[16,256,8,128]{3,1,0,2:T(8,128)(2,1)} copy(bf16[16,256,8,128]{1,3,2,0:T(8,128)(2,1)} %get-tuple-element.26) | data formatting | bytes 16777216
  341.8 11.4 %copy.67 = bf16[16,256,8,128]{3,1,0,2:T(8,128)(2,1)} copy(bf16[16,256,8,128]{1,3,2,0:T(8,128)(2,1)} %get-tuple-element.27) | data formatting | bytes 16777216
  353.2 11.4 %copy.68 = bf16[16,256,8,128]{3,1,0,2:T(8,128)(2,1)} copy(bf16[16,256,8,128]{1,3,2,0:T(8,128)(2,1)} %get-tuple-element.28) | data formatting | bytes 16777216
  364.6 12.3 %fusion = f32[256,8,128,1]{0,2,3,1:T(8,128)S(1)} fusion(bf16[16,256,8,128]{3,1,0,2:T(8,128)(2,1)} %copy.68, bf16[16,256,8,128]{3,1,0,2:T(8,128)(2,1)} %copy.67, bf16[16,256,8,128]{3,1,0,2:T(8,128)(2,1)} %copy.66, bf16[16,384,128]{1,2,0:T(8,128)(2,1)S(1)} %copy.55), kind=kOutput, calls=%fused_computation | convolution fusion | flops 3296722944 | bytes 27787264 | tf_op jit(solution)/shard_map/krbp,kpq->rbq/dot_general | solution.py:102
  376.9 2.4 broadcast_multiply_fusion
  379.3 170.4 %reduce-scatter.2.cloned.1.call-done = f32[4,256,32]{1,2,0:T(8,128)} async-done(((f32[4,256,1024]{1,2,0:T(8,128)}), f32[4,256,32]{1,2,0:T(8,128)}) %reduce-scatter.2.cloned.1.call-update) | async-done | bytes 131088 | tf_op jit(solution)/shard_map/reduce_scatter | solution.py:109
  (22 shorter events, 0.1 us)
Async XLA Ops:
  7.2 4.7 copy-start
  7.2 171.5 %copy-start.6 = (s32[1,256]{1,0:T(1,128)S(1)}, s32[1,256]{1,0:T(1,128)}, u32[]{:S(2)}) copy-start(s32[1,256]{1,0:T(1,128)} %param.17) | copy-start | bytes 3076
  7.2 157.8 %all-gather.2.cloned.1.call-start = ((), (), s32[]{:S(2)}) async-start(), calls=%async_computation.1 | async-start | bytes 2162688 | tf_op jit(solution)/shard_map/all_gather | solution.py:74
  8.8 541.0 %reduce-scatter.2.cloned.1.call-start = ((), (), s32[]{:S(2)}) async-start(), calls=%async_computation.2 | async-start | bytes 4325376 | tf_op jit(solution)/shard_map/reduce_scatter | solution.py:109
  170.7 8.0 %collective-permute-start = (bf16[10,1024]{1,0:T(8,128)(2,1)S(1)}, bf16[10,1024]{1,0:T(8,128)(2,1)S(1)}, u32[]{:S(2)}, u32[]{:S(2)}) collective-permute-start(bf16[10,1024]{1,0:T(8,128)(2,1)S(1)} %get-tuple-element.34), channel_id=1, source_target_pairs={{0,1},{1,2},{2,3},{4,5},{5,6},{6,7},{8,9},{9,10},{10,11},{12,13},{... | collective-permute-start | bytes 61448 | tf_op jit(solution)/shard_map/ppermute | solution.py:15
  172.7 6.7 %collective-permute-start.1 = (bf16[10,1024]{1,0:T(8,128)(2,1)S(1)}, bf16[10,1024]{1,0:T(8,128)(2,1)S(1)}, u32[]{:S(2)}, u32[]{:S(2)}) collective-permute-start(bf16[10,1024]{1,0:T(8,128)(2,1)S(1)} %get-tuple-element.35), channel_id=1, source_target_pairs={{1,0},{2,1},{3,2},{5,4},{6,5},{7,6},{9,8},{10,9},{11,10},{13,12},{... | collective-permute-start | bytes 61448 | tf_op jit(solution)/shard_map/ppermute | solution.py:17
  182.9 1.4 copy-start.3
  213.8 13.0 %copy-start.5 = (bf16[1,256,1024]{2,1,0:T(8,128)(2,1)S(1)}, bf16[1,256,1024]{2,1,0:T(8,128)(2,1)}, u32[]{:S(2)}) copy-start(bf16[1,256,1024]{2,1,0:T(8,128)(2,1)} %param.15) | copy-start | bytes 1572868
  227.0 17.7 %copy-start.2 = (f32[1,256,1024]{2,1,0:T(8,128)}, f32[1,256,1024]{2,1,0:T(8,128)S(1)}, u32[]{:S(2)}) copy-start(f32[1,256,1024]{2,1,0:T(8,128)S(1)} %fusion.31) | copy-start | bytes 3145732
  227.0 22.0 %copy-start.4 = (s32[384,128]{1,0:T(8,128)S(1)}, s32[384,128]{1,0:T(8,128)}, u32[]{:S(2)}) copy-start(s32[384,128]{1,0:T(8,128)} %subtract_add_fusion) | copy-start | bytes 589828
  247.1 22.6 %collective-permute-start.2 = (bf16[16,10,1024]{2,1,0:T(8,128)(2,1)}, bf16[16,10,1024]{2,1,0:T(8,128)(2,1)}, u32[]{:S(2)}, u32[]{:S(2)}) collective-permute-start(bf16[16,10,1024]{2,1,0:T(8,128)(2,1)} %get-tuple-element.30), channel_id=1, source_target_pairs={{0,1},{1,2},{2,3},{4,5},{5,6},{6,7},{8,9},{9,10},{10,11},{12,13},{... | collective-permute-start | bytes 983048 | tf_op jit(solution)/shard_map/ppermute | solution.py:27
  250.1 27.1 %collective-permute-start.3 = (bf16[16,10,1024]{2,1,0:T(8,128)(2,1)}, bf16[16,10,1024]{2,1,0:T(8,128)(2,1)}, u32[]{:S(2)}, u32[]{:S(2)}) collective-permute-start(bf16[16,10,1024]{2,1,0:T(8,128)(2,1)} %get-tuple-element.29), channel_id=1, source_target_pairs={{1,0},{2,1},{3,2},{5,4},{6,5},{7,6},{9,8},{10,9},{11,10},{13,12},{... | collective-permute-start | bytes 983048 | tf_op jit(solution)/shard_map/ppermute | solution.py:27
  376.9 172.8 %copy-start.1 = (bf16[16,21]{1,0:T(8,128)(2,1)S(1)}, bf16[16,21]{1,0:T(8,128)(2,1)}, u32[]{:S(2)}) copy-start(bf16[16,21]{1,0:T(8,128)(2,1)} %param.12) | copy-start | bytes 2020
Sparse Core Ops, SparseCore 0:
  10.2 154.7 all-gather.1
  379.4 170.2 reduce-scatter.1
where the time goes:
time: 559 us; the launch traced here: 557 us
  waiting for transfers between devices  320 us (57%)
  local copies, waits for them, and re-layouts  132 us (24%)
  matrix products  55.8 us (10%)
  other arithmetic  18.3 us (3%)
  between operations  15.9 us (3%)
  starting transfers between devices  14.4 us (3%)
    reduce_scatter x1, waiting for transfers between devices, body(): lax.psum_scatter(selector[:, None, None] * own_term[None], 'exp', scatter...  170 us
    all_gather x1, waiting for transfers between devices, body(): all_cells = lax.all_gather(latent, 'exp', axis=2, tiled=True)  149 us
    unnamed x23, local copies, waits for them, and re-layouts  51.4 us
    convert_element_type x2, local copies, waits for them, and re-layouts, body(): rowblur.reshape(kernel_count, strip_rows + 2 * halfwidth, cell_width)  22.3 us
    dot_general x1, matrix products, body(): jnp.einsum('kyi,kyx->kix', matrix, weighted, preferred_element_type=jnp.f...  17.7 us
    slice x2, local copies, waits for them, and re-layouts, stacked_blocks(): blocked[..., :-2, :]  17 us
    dot_general x1, matrix products, body(): jnp.einsum('kyi,kix->kyx', matrix, rowblur, preferred_element_type=jnp.fl...  13 us
    slice x1, local copies, waits for them, and re-layouts, body(): middle = colback_ext[:, halfwidth:strip_rows + halfwidth]  12.6 us
  transfers between devices with their start and end apart: 6, of which 3 were waited for; matrix products, arithmetic and copies ran while one was open for 5% of the time, Pallas kernels for 0%

commit v1 on v0

v1 whole, which is shorter than its diff:
```python
import jax
import jax.numpy as jnp
from jax import lax
from jax.experimental import pallas as pl
from jax.experimental.pallas import tpu as pltpu
from jax.sharding import PartitionSpec as P

F32 = jnp.float32
BF16 = jnp.bfloat16
KERNELS = 16
PAIRS = KERNELS // 2
TAPS = 21
HALF = TAPS // 2
CELLS = 4
EXPOSURES = 32
ROWS = 256
COLS = 1024
BLOCKS = COLS // 128
OWN = COLS // EXPOSURES
SKY = 32
RIM = 16
LAT = ROWS + 2 * SKY
LATP = 384
EXT = ROWS + 2 * RIM
HOUT = EXT // 2
RBR = HOUT + 256
WR = 384

VMEM = pl.BlockSpec(memory_space=pltpu.VMEM)
SMEM = pl.BlockSpec(memory_space=pltpu.SMEM)
ANY = pl.BlockSpec(memory_space=pl.ANY)


def dot(a, b):
    return lax.dot_general(a, b, (((1,), (0,)), ((), ())), preferred_element_type=F32)


def dot_nt(a, b):
    return lax.dot_general(a, b, (((1,), (1,)), ((), ())), preferred_element_type=F32)


def base_rows(taps, place):
    lane = lax.broadcasted_iota(jnp.int32, (KERNELS, 256), 1)
    out = jnp.zeros((KERNELS, 256), F32)
    for t in range(TAPS):
        out = jnp.where(lane == place(t) % 256, taps[:, t : t + 1], out)
    return out


def skewed(row, count):
    return pltpu.roll(jnp.broadcast_to(row, (count, 256)), 0, 1, stride=1, stride_axis=0).astype(BF16)


def column_of(valid):
    return jnp.broadcast_to(valid, (128, valid.shape[1])).T


def prepare_kernel(row_ref, col_ref, valid_ref, obs_ref, coef_hbm, f_ref, c_ref, a_ref, b_ref, up_ref, down_ref, head, tail, sem):
    head_in = pltpu.make_async_copy(coef_hbm.at[0, :, pl.ds(0, RIM), :], head, sem.at[0])
    tail_in = pltpu.make_async_copy(coef_hbm.at[0, :, pl.ds(ROWS - RIM, RIM), :], tail, sem.at[1])
    head_in.start()
    tail_in.start()
    rows = row_ref[...].astype(F32)
    cols = col_ref[...].astype(F32)
    f_base = base_rows(rows, lambda t: t - HALF)
    b_base = base_rows(rows, lambda t: HALF - t)
    c_base = base_rows(cols, lambda t: t + SKY - RIM - HALF)
    a_base = base_rows(cols, lambda t: RIM + HALF - t)
    for k in range(KERNELS):
        i, q = k // 2, k % 2
        f_ref[i, 128 * q : 128 * q + 128, :] = skewed(f_base[k : k + 1], 128)
        b_ref[i, :, 256 * q : 256 * q + 256] = skewed(b_base[k : k + 1], 128)
        c_ref[k] = skewed(c_base[k : k + 1], HOUT)
        a_ref[k] = skewed(a_base[k : k + 1], 128)
    mask = column_of(valid_ref[...].astype(F32))
    head_mask = jnp.concatenate([mask[:RIM]] * BLOCKS, axis=1)
    tail_mask = jnp.concatenate([mask[ROWS - RIM :]] * BLOCKS, axis=1)
    up_ref[KERNELS] = (obs_ref[0, :RIM, :].astype(F32) * head_mask).astype(BF16)
    down_ref[KERNELS] = (obs_ref[0, ROWS - RIM :, :].astype(F32) * tail_mask).astype(BF16)
    head_in.wait()
    tail_in.wait()
    for k in range(KERNELS):
        up_ref[k] = (head[k].astype(F32) * head_mask).astype(BF16)
        down_ref[k] = (tail[k].astype(F32) * tail_mask).astype(BF16)


def prepare(row_taps, column_taps, valid, observed, coefficients):
    rim = jax.ShapeDtypeStruct((KERNELS + 1, RIM, COLS), BF16)
    return pl.pallas_call(
        prepare_kernel,
        out_shape=(
            jax.ShapeDtypeStruct((PAIRS, 256, 256), BF16),
            jax.ShapeDtypeStruct((KERNELS, HOUT, 256), BF16),
            jax.ShapeDtypeStruct((KERNELS, 128, 256), BF16),
            jax.ShapeDtypeStruct((PAIRS, 128, 512), BF16),
            rim,
            rim,
        ),
        in_specs=[VMEM, VMEM, VMEM, VMEM, ANY],
        out_specs=(VMEM,) * 6,
        scratch_shapes=[
            pltpu.VMEM((KERNELS, RIM, COLS), BF16),
            pltpu.VMEM((KERNELS, RIM, COLS), BF16),
            pltpu.SemaphoreType.DMA((2,)),
        ],
        name="prepare",
    )(row_taps, column_taps, valid, observed, coefficients)


def pack_kernel(cell_ref, lat_ref, above_ref, below_ref, out_ref, turned):
    eye = (
        lax.broadcasted_iota(jnp.int32, (OWN, OWN), 0) == lax.broadcasted_iota(jnp.int32, (OWN, OWN), 1)
    ).astype(BF16)
    for c in range(CELLS):
        turned[c, :, 0:SKY] = dot_nt(eye, above_ref[c]).astype(BF16)
        turned[c, :, SKY : SKY + ROWS] = dot_nt(eye, lat_ref[c]).astype(BF16)
        turned[c, :, SKY + ROWS : LAT] = dot_nt(eye, below_ref[c]).astype(BF16)
        turned[c, :, LAT:] = jnp.zeros((OWN, LATP - LAT), BF16)
    for e in range(EXPOSURES):
        out_ref[e] = turned[cell_ref[e, 0]]


def pack(cell_of, latent, above, below):
    return pl.pallas_call(
        pack_kernel,
        out_shape=jax.ShapeDtypeStruct((EXPOSURES, OWN, LATP), BF16),
        in_specs=[SMEM, VMEM, VMEM, VMEM],
        out_specs=VMEM,
        scratch_shapes=[pltpu.VMEM((CELLS, OWN, LATP), BF16)],
        name="pack",
    )(cell_of, latent, above, below)


def main_kernel(
    strip_ref, valid_ref, f_ref, c_ref, a_ref, b_ref, coef_hbm, obs_hbm, above_hbm, below_hbm,
    res_hbm, send_ref,
    sky, windows, coef, obs, rb, pred, w, cb, acc, sem,
):
    def coef_in(k):
        return pltpu.make_async_copy(coef_hbm.at[0, k], coef.at[k, pl.ds(RIM, ROWS), :], sem.at[k])

    rims = [
        pltpu.make_async_copy(obs_hbm.at[0], obs.at[pl.ds(RIM, ROWS), :], sem.at[KERNELS]),
        pltpu.make_async_copy(above_hbm.at[KERNELS], obs.at[pl.ds(0, RIM), :], sem.at[KERNELS + 1]),
        pltpu.make_async_copy(below_hbm.at[KERNELS], obs.at[pl.ds(RIM + ROWS, RIM), :], sem.at[KERNELS + 2]),
        pltpu.make_async_copy(above_hbm.at[pl.ds(0, KERNELS)], coef.at[:, pl.ds(0, RIM), :], sem.at[KERNELS + 3]),
        pltpu.make_async_copy(
            below_hbm.at[pl.ds(0, KERNELS)], coef.at[:, pl.ds(RIM + ROWS, RIM), :], sem.at[KERNELS + 4]
        ),
    ]
    for copy in rims:
        copy.start()
    for k in range(KERNELS):
        coef_in(k).start()

    low = lax.broadcasted_iota(jnp.int32, (LAT, 128), 1) < 64
    for j in range(BLOCKS):
        sky[j] = strip_ref[128 * j : 128 * j + 128, :].astype(F32).T[:LAT]
    zero = jnp.zeros((LAT, 128), F32)
    for j in range(BLOCKS):
        after = sky[j + 1] if j + 1 < BLOCKS else zero
        before = sky[j - 1] if j > 0 else zero
        windows[j, :, 0:128] = sky[j].astype(BF16)
        windows[j, :, 128:256] = jnp.where(low, after, before).astype(BF16)
    rb[:, LAT:, :] = jnp.zeros((2, RBR - LAT, COLS), BF16)
    w[:, EXT:, :] = jnp.zeros((2, WR - EXT, COLS), BF16)
    for copy in rims:
        copy.wait()
    pred[...] = -obs[...].astype(F32)

    def forward(i, carry):
        f = f_ref[i]
        for j in range(BLOCKS):
            both = dot_nt(windows[j], f)
            rb[0, 0:LAT, 128 * j : 128 * j + 128] = both[:, :128].astype(BF16)
            rb[1, 0:LAT, 128 * j : 128 * j + 128] = both[:, 128:].astype(BF16)
        for q in range(2):
            k = 2 * i + q
            coef_in(k).wait()
            c = c_ref[k]
            for h in range(2):
                out = slice(HOUT * h, HOUT * h + HOUT)
                for x in range(0, COLS, 256):
                    v = dot(c, rb[q, HOUT * h : HOUT * h + 256, x : x + 256])
                    pred[out, x : x + 256] += coef[k, out, x : x + 256].astype(F32) * v
        return carry

    lax.fori_loop(0, PAIRS, forward, 0)

    mask = column_of(valid_ref[...].astype(F32))
    for j in range(BLOCKS):
        pred[RIM : RIM + ROWS, 128 * j : 128 * j + 128] *= mask
    res_out = pltpu.make_async_copy(pred.at[pl.ds(RIM, ROWS), :], res_hbm.at[0], sem.at[KERNELS])
    res_out.start()

    acc[...] = jnp.zeros_like(acc)
    low_y = lax.broadcasted_iota(jnp.int32, (ROWS, 128), 1) < 64
    none = jnp.zeros((ROWS, 128), BF16)

    def adjoint(i, carry):
        for q in range(2):
            k = 2 * i + q
            for x in range(0, COLS, 256):
                w[q, 0:EXT, x : x + 256] = (coef[k, :, x : x + 256].astype(F32) * pred[:, x : x + 256]).astype(BF16)
            a = a_ref[k]
            for h in range(2):
                for x in range(0, COLS, 256):
                    cb[q, 128 * h : 128 * h + 128, x : x + 256] = dot(
                        a, w[q, 128 * h : 128 * h + 256, x : x + 256]
                    ).astype(BF16)
        b = b_ref[i]
        for j in range(BLOCKS):
            parts = []
            for q in range(2):
                after = cb[q, :, 128 * j + 128 : 128 * j + 256] if j + 1 < BLOCKS else none
                before = cb[q, :, 128 * j - 128 : 128 * j] if j > 0 else none
                parts += [cb[q, :, 128 * j : 128 * j + 128], jnp.where(low_y, after, before)]
            acc[j] += dot_nt(b, jnp.concatenate(parts, axis=1))
        return carry

    lax.fori_loop(0, PAIRS, adjoint, 0)
    for j in range(BLOCKS):
        send_ref[128 * j : 128 * j + 128, :] = acc[j].astype(BF16)
    res_out.wait()


def main(strip, valid, bands, coefficients, observed, above, below):
    return pl.pallas_call(
        main_kernel,
        out_shape=(
            jax.ShapeDtypeStruct((1, ROWS, COLS), F32),
            jax.ShapeDtypeStruct((COLS, ROWS), BF16),
        ),
        in_specs=[VMEM] * 6 + [ANY] * 4,
        out_specs=(ANY, VMEM),
        scratch_shapes=[
            pltpu.VMEM((BLOCKS, LAT, 128), F32),
            pltpu.VMEM((BLOCKS, LAT, 256), BF16),
            pltpu.VMEM((KERNELS, EXT, COLS), BF16),
            pltpu.VMEM((EXT, COLS), BF16),
            pltpu.VMEM((2, RBR, COLS), BF16),
            pltpu.VMEM((EXT, COLS), F32),
            pltpu.VMEM((2, WR, COLS), BF16),
            pltpu.VMEM((2, ROWS, COLS), BF16),
            pltpu.VMEM((BLOCKS, 128, ROWS), F32),
            pltpu.SemaphoreType.DMA((KERNELS + 5,)),
        ],
        name="main",
    )(strip, valid, *bands, coefficients, observed, above, below)


def gather_kernel(cell_ref, terms_ref, out_ref, total):
    total[...] = jnp.zeros_like(total)
    for e in range(EXPOSURES):
        total[cell_ref[e, 0]] += terms_ref[e].astype(F32)
    for c in range(CELLS):
        out_ref[c] = total[c].T


def gather(cell_of, terms):
    return pl.pallas_call(
        gather_kernel,
        out_shape=jax.ShapeDtypeStruct((CELLS, ROWS, OWN), F32),
        in_specs=[SMEM, VMEM],
        out_specs=VMEM,
        scratch_shapes=[pltpu.VMEM((CELLS, OWN, ROWS), F32)],
        name="gather",
    )(cell_of, terms)


def body(latent, row_taps, column_taps, coefficients, observed, cell_of, valid_rows):
    count = lax.axis_size("row")
    downward = [(i, i + 1) for i in range(count - 1)]
    upward = [(i + 1, i) for i in range(count - 1)]
    sky_above = lax.ppermute(latent[:, ROWS - SKY :], "row", downward)
    sky_below = lax.ppermute(latent[:, :SKY], "row", upward)
    *bands, head, tail = prepare(row_taps, column_taps, valid_rows, observed, coefficients)
    above = lax.ppermute(tail, "row", downward)
    below = lax.ppermute(head, "row", upward)
    packed = pack(cell_of, latent, sky_above, sky_below)
    strip = lax.all_to_all(packed, "exp", 0, 0, tiled=True).reshape(COLS, LATP)
    residual, send = main(strip, valid_rows, bands, coefficients, observed, above, below)
    terms = lax.all_to_all(send.reshape(EXPOSURES, OWN, ROWS), "exp", 0, 0, tiled=True)
    return gather(cell_of, terms), residual


def solution(mesh):
    placed = (
        P(None, "row", "exp"),
        P(),
        P(),
        P("exp", None, "row", None),
        P("exp", "row", None),
        P(),
        P("exp", "row"),
    )
    return jax.shard_map(
        body,
        mesh=mesh,
        in_specs=placed,
        out_specs=(P(None, "row", "exp"), P("exp", "row", None)),
        check_vma=False,
    )
```

time: 559 us -> 94.1 us (0.17)
  the two profiles are of different devices: /device:TPU:4 before, /device:TPU:1 now
where the time goes in v1:
time: 94.1 us; the launch traced here: 93.5 us
  Pallas kernels  34.8 us (37%)
  starting transfers between devices  24.5 us (26%)
  blocking collectives  16.4 us (17%)
  waiting for transfers between devices  10.6 us (11%)
  local copies, waits for them, and re-layouts  6.52 us (7%)
    pallas_call x1, Pallas kernels, main(): pl.pallas_call(main_kernel, out_shape=(jax.ShapeDtypeStruct((1, ROWS, COL...  24.5 us
    all_to_all x1, blocking collectives, body(): lax.all_to_all(send.reshape(EXPOSURES, OWN, ROWS), 'exp', 0, 0, tiled=True)  16.4 us
    all_to_all x1, starting transfers between devices, body(): strip = lax.all_to_all(packed, 'exp', 0, 0, tiled=True).reshape(COLS, LATP)  8.92 us
    unnamed x15, local copies, waits for them, and re-layouts  6.51 us
    ppermute x1, waiting for transfers between devices, body(): below = lax.ppermute(head, 'row', upward)  5.79 us
    pallas_call x1, Pallas kernels, prepare(): pl.pallas_call(prepare_kernel, out_shape=(jax.ShapeDtypeStruct((PAIRS, 25...  5.72 us
    ppermute x1, starting transfers between devices, body(): above = lax.ppermute(tail, 'row', downward)  5.67 us
    ppermute x1, waiting for transfers between devices, body(): above = lax.ppermute(tail, 'row', downward)  4.84 us
  transfers between devices with their start and end apart: 5, of which 2 were waited for; matrix products, arithmetic and copies ran while one was open for 1% of the time, Pallas kernels for 6%

profile of v1, /device:TPU:1, one launch (start us, length us, event | category | flops | bytes accessed | tf_op | source)
XLA Modules:
  0.0 93.5 jit_solution(3167235068112366296)
XLA Ops:
  0.6 1.0 %copy.12.lat_ref = bf16[4,256,32]{2,1,0:T(8,128)(2,1)S(1)} copy(bf16[4,256,32]{1,2,0:T(8,128)(2,1)} %param.7) | data formatting | bytes 131072 | tf_op args[0]
  1.6 0.0 copy-start.1
  1.7 3.3 %collective-permute-start.1 = (bf16[4,32,32]{2,1,0:T(8,128)(2,1)S(1)}, bf16[4,32,32]{2,1,0:T(8,128)(2,1)S(1)}, u32[]{:S(2)}, u32[]{:S(2)}) collective-permute-start(bf16[4,32,32]{2,1,0:T(8,128)(2,1)S(1)} %get-tuple-element.20), channel_id=1, source_target_pairs={{1,0},{2,1},{3,2},{5,4},{6,5},{7,6},{9,8},{10,9},{11,10},{13,12},{... | collective-permute-start | bytes 24584 | tf_op jit(solution)/shard_map/ppermute | solution.py:276
  5.0 4.7 %collective-permute-start = (bf16[4,32,32]{2,1,0:T(8,128)(2,1)S(1)}, bf16[4,32,32]{2,1,0:T(8,128)(2,1)S(1)}, u32[]{:S(2)}, u32[]{:S(2)}) collective-permute-start(bf16[4,32,32]{2,1,0:T(8,128)(2,1)S(1)} %get-tuple-element.21), channel_id=1, source_target_pairs={{0,1},{1,2},{2,3},{4,5},{5,6},{6,7},{8,9},{9,10},{10,11},{12,13},{... | collective-permute-start | bytes 24584 | tf_op jit(solution)/shard_map/ppermute | solution.py:275
  9.6 1.3 %copy.13.cell_ref = s32[32,1]{1,0:T(8,128)} copy(s32[32,1]{0,1:T(1,128)} %param.12) | data formatting | bytes 256 | tf_op args[5]
  11.0 0.0 collective-permute-done.1.below_ref
  11.0 0.0 copy-start.4
  11.0 0.0 collective-permute-done.above_ref
  11.0 0.0 copy-done.1
  11.0 0.6 copy-done.4
  11.6 0.0 copy-start.5
  11.6 0.6 copy-done.5
  12.2 2.3 %pack.1 = bf16[32,32,384]{2,1,0:T(8,128)(2,1)} custom-call(s32[32,1]{1,0:T(8,128)} %copy.13.cell_ref, bf16[4,256,32]{2,1,0:T(8,128)(2,1)} %copy-done.1, bf16[4,32,32]{2,1,0:T(8,128)(2,1)} %copy-done.5, bf16[4,32,32]{2,1,0:T(8,128)(2,1)} %copy-done.4), custom_call_target="tpu_custom_call" | custom-call | tf_op jit(solution)/shard_map/pack/pallas_call | solution.py:124
  14.5 8.9 %all-to-all-start = ((bf16[32,32,384]{2,1,0:T(8,128)(2,1)}), bf16[32,32,384]{2,1,0:T(8,128)(2,1)S(1)}, u32[]{:S(2)}, u32[]{:S(2)}) async-start(bf16[32,32,384]{2,1,0:T(8,128)(2,1)} %pack.1), calls=%async_computation | async-start | bytes 1572864 | tf_op jit(solution)/shard_map/all_to_all | solution.py:281
  23.4 5.7 %prepare.1 = (bf16[8,256,256]{2,1,0:T(8,128)(2,1)}, bf16[16,144,256]{2,1,0:T(8,128)(2,1)}, bf16[16,128,256]{2,1,0:T(8,128)(2,1)}, bf16[8,128,512]{2,1,0:T(8,128)...) custom-call(bf16[16,21]{1,0:T(8,128)(2,1)} %row_ref.1, bf16[16,21]{1,0:T(8,128)(2,1)} %col_ref.1, ...), custom_call_target="tpu_custom_call" | custom-call | tf_op jit(solution)/shard_map/prepare/pallas_call | solution.py:89
  29.2 5.7 %collective-permute-start.2 = (bf16[17,16,1024]{2,1,0:T(8,128)(2,1)}, bf16[17,16,1024]{2,1,0:T(8,128)(2,1)S(1)}, u32[]{:S(2)}, u32[]{:S(2)}) collective-permute-start(bf16[17,16,1024]{2,1,0:T(8,128)(2,1)} %get-tuple-element.14), channel_id=1, source_target_pairs={{0,1},{1,2},{2,3},{4,5},{5,6},{6,7},{8,9},{9,10},{10,11},{12,13},{... | collective-permute-start | bytes 1671176 | tf_op jit(solution)/shard_map/ppermute | solution.py:278
  34.8 1.9 %collective-permute-start.3 = (bf16[17,16,1024]{2,1,0:T(8,128)(2,1)}, bf16[17,16,1024]{2,1,0:T(8,128)(2,1)S(1)}, u32[]{:S(2)}, u32[]{:S(2)}) collective-permute-start(bf16[17,16,1024]{2,1,0:T(8,128)(2,1)} %get-tuple-element.15), channel_id=1, source_target_pairs={{1,0},{2,1},{3,2},{5,4},{6,5},{7,6},{9,8},{10,9},{11,10},{13,12},{... | collective-permute-start | bytes 1671176 | tf_op jit(solution)/shard_map/ppermute | solution.py:279
  36.8 4.8 %collective-permute-done.2.above_hbm = bf16[17,16,1024]{2,1,0:T(8,128)(2,1)S(1)} collective-permute-done((bf16[17,16,1024]{2,1,0:T(8,128)(2,1)}, bf16[17,16,1024]{2,1,0:T(8,128)(2,1)S(1)}, u32[]{:S(2)}, u32[]{:S(2)}) %collective-permute-start.2) | collective-permute-done | bytes 557088 | tf_op jit(solution)/shard_map/ppermute | solution.py:278
  41.6 0.0 copy-start.2
  41.6 5.8 %collective-permute-done.3.below_hbm = bf16[17,16,1024]{2,1,0:T(8,128)(2,1)S(1)} collective-permute-done((bf16[17,16,1024]{2,1,0:T(8,128)(2,1)}, bf16[17,16,1024]{2,1,0:T(8,128)(2,1)S(1)}, u32[]{:S(2)}, u32[]{:S(2)}) %collective-permute-start.3) | collective-permute-done | bytes 557088 | tf_op jit(solution)/shard_map/ppermute | solution.py:279
  47.4 0.0 copy-start.3
  47.4 0.0 all-to-all-done
  47.4 0.0 copy-start
  47.4 0.0 copy-done.2
  47.4 0.8 copy-done.3
  48.2 0.3 copy-done
  48.5 24.5 %main.1 = (f32[1,256,1024]{2,1,0:T(8,128)}, bf16[1024,256]{1,0:T(8,128)(2,1)}) custom-call(bf16[1024,384]{1,0:T(8,128)(2,1)} %bitcast.2, s32[1,256]{1,0:T(1,128)} %valid_ref.3, bf16[8,256,256]{2,1,0:T(8,128)(2,1)} %get-tuple-element.10.f_ref, bf16[16,144,256]{2,1,0:T(8,128)(2,1)} %get-tuple-element.11.c_ref, bf16[16,128,256]{2,1,0:T(8,128)(2,1)} %get-tuple-element.12.a_ref, ...), custom_call_target="tpu_custom_call" | custom-call | tf_op jit(solution)/shard_map/main/pallas_call | solution.py:228
  73.0 16.4 %all_to_all.10.terms_ref = bf16[32,32,256]{2,1,0:T(8,128)(2,1)} all-to-all(bf16[32,32,256]{2,1,0:T(8,128)(2,1)} %bitcast.3), channel_id=1, replica_groups=mesh['exp'=32,'row'=4] {'exp'}, dimensions={0} | all-to-all | bytes 1048576 | tf_op jit(solution)/shard_map/all_to_all | solution.py:283
  89.4 2.2 %gather.1 = f32[4,256,32]{2,1,0:T(8,128)} custom-call(s32[32,1]{1,0:T(8,128)} %copy.13.cell_ref, bf16[32,32,256]{2,1,0:T(8,128)(2,1)} %all_to_all.10.terms_ref), custom_call_target="tpu_custom_call" | custom-call | tf_op jit(solution)/shard_map/gather/pallas_call | solution.py:261
  91.6 1.9 %copy.14 = f32[4,256,32]{1,2,0:T(8,128)} copy(f32[4,256,32]{2,1,0:T(8,128)} %gather.1) | data formatting | bytes 262144
  (1 shorter events, 0.0 us)
Async XLA Ops:
  1.6 9.3 %copy-start.1 = (bf16[4,256,32]{2,1,0:T(8,128)(2,1)}, bf16[4,256,32]{2,1,0:T(8,128)(2,1)S(1)}, u32[]{:S(2)}) copy-start(bf16[4,256,32]{2,1,0:T(8,128)(2,1)S(1)} %copy.12.lat_ref) | copy-start | bytes 196612
  1.7 9.3 %collective-permute-start.1 = (bf16[4,32,32]{2,1,0:T(8,128)(2,1)S(1)}, bf16[4,32,32]{2,1,0:T(8,128)(2,1)S(1)}, u32[]{:S(2)}, u32[]{:S(2)}) collective-permute-start(bf16[4,32,32]{2,1,0:T(8,128)(2,1)S(1)} %get-tuple-element.20), channel_id=1, source_target_pairs={{1,0},{2,1},{3,2},{5,4},{6,5},{7,6},{9,8},{10,9},{11,10},{13,12},{... | collective-permute-start | bytes 24584 | tf_op jit(solution)/shard_map/ppermute | solution.py:276
  5.0 6.0 %collective-permute-start = (bf16[4,32,32]{2,1,0:T(8,128)(2,1)S(1)}, bf16[4,32,32]{2,1,0:T(8,128)(2,1)S(1)}, u32[]{:S(2)}, u32[]{:S(2)}) collective-permute-start(bf16[4,32,32]{2,1,0:T(8,128)(2,1)S(1)} %get-tuple-element.21), channel_id=1, source_target_pairs={{0,1},{1,2},{2,3},{4,5},{5,6},{6,7},{8,9},{9,10},{10,11},{12,13},{... | collective-permute-start | bytes 24584 | tf_op jit(solution)/shard_map/ppermute | solution.py:275
  11.0 0.6 copy-start.4
  11.6 0.6 copy-start.5
  14.5 32.9 %all-to-all-start = ((bf16[32,32,384]{2,1,0:T(8,128)(2,1)}), bf16[32,32,384]{2,1,0:T(8,128)(2,1)S(1)}, u32[]{:S(2)}, u32[]{:S(2)}) async-start(bf16[32,32,384]{2,1,0:T(8,128)(2,1)} %pack.1), calls=%async_computation | async-start | bytes 1572864 | tf_op jit(solution)/shard_map/all_to_all | solution.py:281
  29.2 12.4 %collective-permute-start.2 = (bf16[17,16,1024]{2,1,0:T(8,128)(2,1)}, bf16[17,16,1024]{2,1,0:T(8,128)(2,1)S(1)}, u32[]{:S(2)}, u32[]{:S(2)}) collective-permute-start(bf16[17,16,1024]{2,1,0:T(8,128)(2,1)} %get-tuple-element.14), channel_id=1, source_target_pairs={{0,1},{1,2},{2,3},{4,5},{5,6},{6,7},{8,9},{9,10},{10,11},{12,13},{... | collective-permute-start | bytes 1671176 | tf_op jit(solution)/shard_map/ppermute | solution.py:278
  34.8 12.6 %collective-permute-start.3 = (bf16[17,16,1024]{2,1,0:T(8,128)(2,1)}, bf16[17,16,1024]{2,1,0:T(8,128)(2,1)S(1)}, u32[]{:S(2)}, u32[]{:S(2)}) collective-permute-start(bf16[17,16,1024]{2,1,0:T(8,128)(2,1)} %get-tuple-element.15), channel_id=1, source_target_pairs={{1,0},{2,1},{3,2},{5,4},{6,5},{7,6},{9,8},{10,9},{11,10},{13,12},{... | collective-permute-start | bytes 1671176 | tf_op jit(solution)/shard_map/ppermute | solution.py:279
  41.6 5.8 %copy-start.2 = (bf16[17,16,1024]{2,1,0:T(8,128)(2,1)}, bf16[17,16,1024]{2,1,0:T(8,128)(2,1)S(1)}, u32[]{:S(2)}) copy-start(bf16[17,16,1024]{2,1,0:T(8,128)(2,1)S(1)} %collective-permute-done.2.above_hbm) | copy-start | bytes 1671172
  47.4 0.8 copy-start.3
  47.4 1.1 %copy-start = (bf16[32,32,384]{2,1,0:T(8,128)(2,1)}, bf16[32,32,384]{2,1,0:T(8,128)(2,1)S(1)}, u32[]{:S(2)}) copy-start(bf16[32,32,384]{2,1,0:T(8,128)(2,1)S(1)} %all-to-all-done) | copy-start | bytes 2359300

commit v2 on v1

v2 whole, which is shorter than its diff:
```python
import jax
import jax.numpy as jnp
from jax import lax
from jax.experimental import pallas as pl
from jax.experimental.pallas import tpu as pltpu
from jax.sharding import PartitionSpec as P

F32 = jnp.float32
BF16 = jnp.bfloat16
KERNELS = 16
PAIRS = KERNELS // 2
TAPS = 21
HALF = TAPS // 2
CELLS = 4
EXPOSURES = 32
ROWS = 256
COLS = 1024
BLOCKS = COLS // 128
OWN = COLS // EXPOSURES
SKY = 24
RIM = 16
LAT = ROWS + 2 * SKY
LATP = 384
EXT = ROWS + 2 * RIM
HOUT = EXT // 2
TOP = 8
RBR = HOUT + 256
WR = 384

VMEM = pl.BlockSpec(memory_space=pltpu.VMEM)
SMEM = pl.BlockSpec(memory_space=pltpu.SMEM)
ANY = pl.BlockSpec(memory_space=pl.ANY)


def dot(a, b):
    return lax.dot_general(a, b, (((1,), (0,)), ((), ())), preferred_element_type=F32)


def column_of(valid):
    return jnp.broadcast_to(valid, (128, valid.shape[1])).T


def rims_kernel(valid_ref, obs_hbm, coef_hbm, up_ref, down_ref, head, tail, sem):
    copies = [
        pltpu.make_async_copy(coef_hbm.at[0, :, pl.ds(0, RIM), :], head.at[pl.ds(0, KERNELS)], sem.at[0]),
        pltpu.make_async_copy(coef_hbm.at[0, :, pl.ds(ROWS - RIM, RIM), :], tail.at[pl.ds(0, KERNELS)], sem.at[1]),
        pltpu.make_async_copy(obs_hbm.at[0, pl.ds(0, RIM), :], head.at[KERNELS], sem.at[2]),
        pltpu.make_async_copy(obs_hbm.at[0, pl.ds(ROWS - RIM, RIM), :], tail.at[KERNELS], sem.at[3]),
    ]
    for copy in copies:
        copy.start()
    mask = column_of(valid_ref[...].astype(F32))
    head_mask = jnp.concatenate([mask[:RIM]] * BLOCKS, axis=1)
    tail_mask = jnp.concatenate([mask[ROWS - RIM :]] * BLOCKS, axis=1)
    for copy in copies:
        copy.wait()
    for k in range(KERNELS + 1):
        up_ref[k] = (head[k].astype(F32) * head_mask).astype(BF16)
        down_ref[k] = (tail[k].astype(F32) * tail_mask).astype(BF16)


def rims(valid, observed, coefficients):
    rim = (KERNELS + 1, RIM, COLS)
    return pl.pallas_call(
        rims_kernel,
        out_shape=(jax.ShapeDtypeStruct(rim, BF16),) * 2,
        in_specs=[VMEM, ANY, ANY],
        out_specs=(VMEM,) * 2,
        scratch_shapes=[pltpu.VMEM(rim, BF16), pltpu.VMEM(rim, BF16), pltpu.SemaphoreType.DMA((4,))],
        name="rims",
    )(valid, observed, coefficients)


def base_rows(taps, place):
    lane = lax.broadcasted_iota(jnp.int32, (KERNELS, 256), 1)
    out = jnp.zeros((KERNELS, 256), F32)
    for t in range(TAPS):
        out = jnp.where(lane == place(t) % 256, taps[:, t : t + 1], out)
    return out


def skewed(row, count):
    return pltpu.roll(jnp.broadcast_to(row, (count, 256)), 0, 1, stride=1, stride_axis=0)


def bands_kernel(row_ref, col_ref, f_ref, c_ref, a_ref, b_ref):
    rows = row_ref[...].astype(F32)
    cols = col_ref[...].astype(F32)
    f_base = base_rows(rows, lambda t: HALF - t)
    b_base = base_rows(rows, lambda t: t - HALF)
    c_base = base_rows(cols, lambda t: t + 2 * RIM - RIM - HALF)
    a_base = base_rows(cols, lambda t: RIM + HALF - t)
    at = lax.broadcasted_iota(jnp.int32, (256, 256), 0)
    out = lax.broadcasted_iota(jnp.int32, (256, 256), 1)
    near = jnp.abs(at - out) < 128
    for k in range(KERNELS):
        i, q = k // 2, k % 2
        f_ref[i, :, 128 * q : 128 * q + 128] = skewed(f_base[k : k + 1], 256)[:, :128].astype(BF16)
        b = skewed(b_base[k : k + 1], 256)
        b_ref[i, 256 * q : 256 * q + 256, :] = jnp.where(near, b, 0.0).astype(BF16)
        far = jnp.where(near, 0.0, b).astype(BF16)
        b_ref[i, 512 + 128 * q : 576 + 128 * q, :] = far[:64]
        b_ref[i, 576 + 128 * q : 640 + 128 * q, :] = far[192:]
        c_ref[k] = skewed(c_base[k : k + 1], HOUT).astype(BF16)
        a_ref[k] = skewed(a_base[k : k + 1], 128).astype(BF16)


def make_bands(row_taps, column_taps):
    return pl.pallas_call(
        bands_kernel,
        out_shape=(
            jax.ShapeDtypeStruct((PAIRS, 256, 256), BF16),
            jax.ShapeDtypeStruct((KERNELS, HOUT, 256), BF16),
            jax.ShapeDtypeStruct((KERNELS, 128, 256), BF16),
            jax.ShapeDtypeStruct((PAIRS, 768, 256), BF16),
        ),
        in_specs=[VMEM, VMEM],
        out_specs=(VMEM,) * 4,
        name="bands",
    )(row_taps, column_taps)


def pack_kernel(cell_ref, lat_ref, above_ref, below_ref, after_ref, out_ref, turned):
    for c in range(CELLS):
        turned[c] = jnp.concatenate(
            [above_ref[c], lat_ref[c], below_ref[c], jnp.zeros((OWN, LATP - LAT), BF16)], axis=1
        )
    for e in range(EXPOSURES):
        out_ref[e] = turned[cell_ref[0, e]]


def pack(cell_of, latent, above, below, after):
    return pl.pallas_call(
        pack_kernel,
        out_shape=jax.ShapeDtypeStruct((EXPOSURES, OWN, LATP), BF16),
        in_specs=[SMEM, VMEM, VMEM, VMEM, ANY],
        out_specs=VMEM,
        scratch_shapes=[pltpu.VMEM((CELLS, OWN, LATP), BF16)],
        name="pack",
    )(cell_of, latent, above, below, after)


def main_kernel(
    strip_hbm, valid_ref, f_hbm, c_hbm, a_hbm, b_hbm, coef_hbm, obs_hbm, above_hbm, below_hbm,
    res_hbm, send_ref,
    strip_ref, f_ref, c_ref, a_ref, b_ref, sky, windows, coef, obs, rb, rb2, pred, w, w2, cb, cb2, acc, sem, rim_sem, band_sem,
):
    def coef_in(k):
        return pltpu.make_async_copy(coef_hbm.at[0, k], coef.at[k, pl.ds(RIM, ROWS), :], sem.at[k])

    pairs = ((f_hbm, f_ref), (c_hbm, c_ref), (a_hbm, a_ref), (b_hbm, b_ref), (strip_hbm, strip_ref))
    f_in, c_in, a_in, b_in, strip_in = (
        pltpu.make_async_copy(s, d, band_sem.at[n]) for n, (s, d) in enumerate(pairs)
    )
    rims_in = [
        pltpu.make_async_copy(obs_hbm.at[0], obs.at[pl.ds(RIM, ROWS), :], rim_sem.at[0]),
        pltpu.make_async_copy(above_hbm.at[KERNELS], obs.at[pl.ds(0, RIM), :], rim_sem.at[1]),
        pltpu.make_async_copy(below_hbm.at[KERNELS], obs.at[pl.ds(RIM + ROWS, RIM), :], rim_sem.at[2]),
        pltpu.make_async_copy(above_hbm.at[pl.ds(0, KERNELS)], coef.at[:, pl.ds(0, RIM), :], rim_sem.at[3]),
        pltpu.make_async_copy(
            below_hbm.at[pl.ds(0, KERNELS)], coef.at[:, pl.ds(RIM + ROWS, RIM), :], rim_sem.at[4]
        ),
    ]
    strip_in.start()
    for copy in rims_in[:3]:
        copy.start()
    f_in.start()
    for copy in rims_in[3:]:
        copy.start()
    c_in.start()
    for k in range(KERNELS):
        coef_in(k).start()
    a_in.start()
    b_in.start()

    for r in (rb, rb2):
        r[:, :, 0:TOP, :] = jnp.zeros((2, BLOCKS, TOP, 128), BF16)
        r[:, :, TOP + LAT :, :] = jnp.zeros((2, BLOCKS, RBR - LAT - TOP, 128), BF16)
    for r in (w, w2):
        r[:, :, EXT:, :] = jnp.zeros((2, BLOCKS, WR - EXT, 128), BF16)
    acc[...] = jnp.zeros_like(acc)
    low = lax.broadcasted_iota(jnp.int32, (LAT, 128), 1) < 64
    strip_in.wait()
    for j in range(BLOCKS):
        sky[j] = strip_ref[128 * j : 128 * j + 128, :].astype(F32).T[:LAT]
    zero = jnp.zeros((LAT, 128), F32)
    for j in range(BLOCKS):
        after = sky[j + 1] if j + 1 < BLOCKS else zero
        before = sky[j - 1] if j > 0 else zero
        windows[j, :, 0:128] = sky[j].astype(BF16)
        windows[j, :, 128:256] = jnp.where(low, after, before).astype(BF16)
    for copy in rims_in[:3]:
        copy.wait()
    pred[...] = -obs[...].astype(F32)
    f_in.wait()
    for copy in rims_in[3:]:
        copy.wait()
    c_in.wait()

    def blur(i, rb):
        f = f_ref[i]
        for j in range(BLOCKS):
            both = dot(windows[j], f)
            rb[0, j, TOP : TOP + LAT, :] = both[:, :128].astype(BF16)
            rb[1, j, TOP : TOP + LAT, :] = both[:, 128:].astype(BF16)

    def predict(i, rb):
        for q in range(2):
            k = 2 * i + q
            c = c_ref[k]
            for h in range(2):
                out = slice(HOUT * h, HOUT * h + HOUT)
                for x in range(0, BLOCKS, 2):
                    at = slice(HOUT * h, HOUT * h + 256)
                    v = dot(c, jnp.concatenate([rb[q, x, at, :], rb[q, x + 1, at, :]], axis=1))
                    cols = slice(128 * x, 128 * x + 256)
                    pred[out, cols] += coef[k, out, cols].astype(F32) * v

    def forward(n, carry):
        for m in range(4):
            coef_in(4 * n + m).wait()
        blur(2 * n, rb)
        blur(2 * n + 1, rb2)
        predict(2 * n, rb)
        predict(2 * n + 1, rb2)
        return carry

    lax.fori_loop(0, PAIRS // 2, forward, 0)

    mask = column_of(valid_ref[...].astype(F32))
    for j in range(BLOCKS):
        pred[RIM : RIM + ROWS, 128 * j : 128 * j + 128] *= mask
    res_out = pltpu.make_async_copy(pred.at[pl.ds(RIM, ROWS), :], res_hbm.at[0], rim_sem.at[0])
    res_out.start()

    low_y = lax.broadcasted_iota(jnp.int32, (ROWS, 128), 1) < 64
    none = jnp.zeros((ROWS, 128), BF16)
    a_in.wait()
    b_in.wait()

    def weigh(i, w):
        for q in range(2):
            for x in range(BLOCKS):
                cols = slice(128 * x, 128 * x + 128)
                w[q, x, 0:EXT, :] = (coef[2 * i + q, :, cols].astype(F32) * pred[:, cols]).astype(BF16)

    def back(i, w, cb):
        for q in range(2):
            a = a_ref[2 * i + q]
            for h in range(2):
                for x in range(0, BLOCKS, 2):
                    at = slice(128 * h, 128 * h + 256)
                    both = dot(a, jnp.concatenate([w[q, x, at, :], w[q, x + 1, at, :]], axis=1))
                    cb[q, x, 128 * h : 128 * h + 128, :] = both[:, :128].astype(BF16)
                    cb[q, x + 1, 128 * h : 128 * h + 128, :] = both[:, 128:].astype(BF16)
        b = b_ref[i]
        for x in range(0, BLOCKS, 2):
            parts = [cb[0, x], cb[0, x + 1], cb[1, x], cb[1, x + 1]]
            for q in range(2):
                after = cb[q, x + 2] if x + 2 < BLOCKS else none
                before = cb[q, x - 1] if x > 0 else none
                parts.append(jnp.where(low_y, after, before))
            acc[x // 2] += dot(jnp.concatenate(parts, axis=1), b)

    weigh(0, w)

    def adjoint(n, carry):
        weigh(2 * n + 1, w2)
        back(2 * n, w, cb)
        weigh(jnp.minimum(2 * n + 2, PAIRS - 1), w)
        back(2 * n + 1, w2, cb2)
        return carry

    lax.fori_loop(0, PAIRS // 2, adjoint, 0)
    for x in range(BLOCKS // 2):
        send_ref[256 * x : 256 * x + 256, :] = acc[x].T.astype(BF16)
    res_out.wait()


def main(strip, valid, bands, coefficients, observed, above, below):
    return pl.pallas_call(
        main_kernel,
        out_shape=(
            jax.ShapeDtypeStruct((1, ROWS, COLS), F32),
            jax.ShapeDtypeStruct((COLS, ROWS), BF16),
        ),
        in_specs=[ANY, VMEM] + [ANY] * 8,
        out_specs=(ANY, VMEM),
        scratch_shapes=[
            pltpu.VMEM((COLS, LATP), BF16),
            pltpu.VMEM((PAIRS, 256, 256), BF16),
            pltpu.VMEM((KERNELS, HOUT, 256), BF16),
            pltpu.VMEM((KERNELS, 128, 256), BF16),
            pltpu.VMEM((PAIRS, 768, 256), BF16),
            pltpu.VMEM((BLOCKS, LAT, 128), F32),
            pltpu.VMEM((BLOCKS, LAT, 256), BF16),
            pltpu.VMEM((KERNELS, EXT, COLS), BF16),
            pltpu.VMEM((EXT, COLS), BF16),
            pltpu.VMEM((2, BLOCKS, RBR, 128), BF16),
            pltpu.VMEM((2, BLOCKS, RBR, 128), BF16),
            pltpu.VMEM((EXT, COLS), F32),
            pltpu.VMEM((2, BLOCKS, WR, 128), BF16),
            pltpu.VMEM((2, BLOCKS, WR, 128), BF16),
            pltpu.VMEM((2, BLOCKS, ROWS, 128), BF16),
            pltpu.VMEM((2, BLOCKS, ROWS, 128), BF16),
            pltpu.VMEM((BLOCKS // 2, ROWS, 256), F32),
            pltpu.SemaphoreType.DMA((KERNELS,)),
            pltpu.SemaphoreType.DMA((5,)),
            pltpu.SemaphoreType.DMA((5,)),
        ],
        name="main",
    )(strip, valid, *bands, coefficients, observed, above, below)


def gather_kernel(cell_ref, terms_ref, out_ref):
    out_ref[...] = jnp.zeros_like(out_ref)
    for e in range(EXPOSURES):
        out_ref[cell_ref[0, e]] += terms_ref[e].astype(F32)


def gather(cell_of, terms):
    return pl.pallas_call(
        gather_kernel,
        out_shape=jax.ShapeDtypeStruct((CELLS, OWN, ROWS), F32),
        in_specs=[SMEM, VMEM],
        out_specs=VMEM,
        name="gather",
    )(cell_of, terms)


def body(latent, row_taps, column_taps, coefficients, observed, cell_of, valid_rows):
    count = lax.axis_size("row")
    downward = [(i, i + 1) for i in range(count - 1)]
    upward = [(i + 1, i) for i in range(count - 1)]
    cell_of = cell_of.reshape(1, EXPOSURES)
    latent = jnp.swapaxes(latent, 1, 2)
    sky_above = lax.ppermute(latent[:, :, ROWS - SKY :], "row", downward)
    sky_below = lax.ppermute(latent[:, :, :SKY], "row", upward)
    head, tail = rims(valid_rows, observed, coefficients)
    above = lax.ppermute(tail, "row", downward)
    below = lax.ppermute(head, "row", upward)
    packed = pack(cell_of, latent, sky_above, sky_below, head)
    bands = make_bands(row_taps, column_taps)
    strip = lax.all_to_all(packed, "exp", 0, 0, tiled=True).reshape(COLS, LATP)
    residual, send = main(strip, valid_rows, bands, coefficients, observed, above, below)
    terms = lax.all_to_all(send.reshape(EXPOSURES, OWN, ROWS), "exp", 0, 0, tiled=True)
    return jnp.swapaxes(gather(cell_of, terms), 1, 2), residual


def solution(mesh):
    placed = (
        P(None, "row", "exp"),
        P(),
        P(),
        P("exp", None, "row", None),
        P("exp", "row", None),
        P(),
        P("exp", "row"),
    )
    return jax.shard_map(
        body,
        mesh=mesh,
        in_specs=placed,
        out_specs=(P(None, "row", "exp"), P("exp", "row", None)),
        check_vma=False,
    )
```

time: 94.1 us -> 81 us (0.86)
  waiting for transfers between devices: 10.6 us -> 5.93 us
  local copies, waits for them, and re-layouts: 6.52 us -> 2.58 us
  Pallas kernels: 34.8 us -> 31.5 us
  starting transfers between devices: 24.5 us -> 23.3 us
    unnamed x15 -> x10, local copies, waits for them, and re-layouts: 6.51 us -> 1.73 us
    pallas_call x1, Pallas kernels: 24.5 us -> 19.9 us  [main(): pl.pallas_call(main_kernel, out_shape=(jax.ShapeDtypeStruct((1, ROWS, COL...]
    ppermute x1, waiting for transfers between devices: 4.84 us -> 2.23 us  [body(): above = lax.ppermute(tail, 'row', downward)]
    ppermute x1, waiting for transfers between devices: 5.79 us -> 3.7 us  [body(): below = lax.ppermute(head, 'row', upward)]
    pallas_call x2 -> x3, Pallas kernels: 7.94 us -> 9.66 us  [the longest x1 4.71 us: make_bands(): pl.pallas_call(bands_kernel, out_shape=(jax.ShapeDtypeStruct((PAIRS, 256,...]
    ppermute x1, starting transfers between devices: 5.67 us -> 4.5 us  [body(): above = lax.ppermute(tail, 'row', downward)]
  transfers between devices with their start and end apart: 5 -> 5, of which waited for: 2 -> 2; matrix products, arithmetic and copies ran while one was open for 1% -> 0% of each run, Pallas kernels for 6% -> 10%
where the time goes in v2:
time: 81 us; the launch traced here: 80.4 us
  Pallas kernels  31.5 us (39%)
  starting transfers between devices  23.3 us (29%)
  blocking collectives  16.4 us (20%)
  waiting for transfers between devices  5.93 us (7%)
  local copies, waits for them, and re-layouts  2.58 us (3%)
    pallas_call x1, Pallas kernels, main(): pl.pallas_call(main_kernel, out_shape=(jax.ShapeDtypeStruct((1, ROWS, COL...  19.9 us
    all_to_all x1, blocking collectives, body(): lax.all_to_all(send.reshape(EXPOSURES, OWN, ROWS), 'exp', 0, 0, tiled=True)  16.4 us
    all_to_all x1, starting transfers between devices, body(): strip = lax.all_to_all(packed, 'exp', 0, 0, tiled=True).reshape(COLS, LATP)  8.91 us
    pallas_call x1, Pallas kernels, make_bands(): pl.pallas_call(bands_kernel, out_shape=(jax.ShapeDtypeStruct((PAIRS, 256,...  4.71 us
    ppermute x1, starting transfers between devices, body(): sky_above = lax.ppermute(latent[:, :, ROWS - SKY:], 'row', downward)  4.66 us
    ppermute x1, starting transfers between devices, body(): above = lax.ppermute(tail, 'row', downward)  4.5 us
    ppermute x1, waiting for transfers between devices, body(): below = lax.ppermute(head, 'row', upward)  3.7 us
    ppermute x1, starting transfers between devices, body(): sky_below = lax.ppermute(latent[:, :, :SKY], 'row', upward)  3.28 us
  transfers between devices with their start and end apart: 5, of which 2 were waited for; matrix products, arithmetic and copies ran while one was open for 0% of the time, Pallas kernels for 10%

profile of v2, /device:TPU:1, one launch (start us, length us, event | category | flops | bytes accessed | tf_op | source)
XLA Modules:
  0.0 80.4 jit_solution(16958648736820909741)
XLA Ops:
  0.6 0.9 %fusion = (bf16[4,32,24]{2,1,0:T(8,128)(2,1)S(1)}, bf16[4,32,24]{2,1,0:T(8,128)(2,1)S(1)}) fusion(bf16[4,32,256]{2,1,0:T(8,128)(2,1)} %bitcast.7), kind=kLoop, calls=%fused_computation | loop fusion | bytes 24576 | tf_op jit(solution)/shard_map/slice | solution.py:338
  1.5 3.3 %collective-permute-start.1 = (bf16[4,32,24]{2,1,0:T(8,128)(2,1)S(1)}, bf16[4,32,24]{2,1,0:T(8,128)(2,1)S(1)}, u32[]{:S(2)}, u32[]{:S(2)}) collective-permute-start(bf16[4,32,24]{2,1,0:T(8,128)(2,1)S(1)} %get-tuple-element.18), channel_id=1, source_target_pairs={{1,0},{2,1},{3,2},{5,4},{6,5},{7,6},{9,8},{10,9},{11,10},{13,12},{... | collective-permute-start | bytes 18440 | tf_op jit(solution)/shard_map/ppermute | solution.py:338
  4.8 4.7 %collective-permute-start = (bf16[4,32,24]{2,1,0:T(8,128)(2,1)S(1)}, bf16[4,32,24]{2,1,0:T(8,128)(2,1)S(1)}, u32[]{:S(2)}, u32[]{:S(2)}) collective-permute-start(bf16[4,32,24]{2,1,0:T(8,128)(2,1)S(1)} %get-tuple-element.19), channel_id=1, source_target_pairs={{0,1},{1,2},{2,3},{4,5},{5,6},{6,7},{8,9},{9,10},{10,11},{12,13},{... | collective-permute-start | bytes 18440 | tf_op jit(solution)/shard_map/ppermute | solution.py:337
  9.4 3.1 %rims.1 = (bf16[17,16,1024]{2,1,0:T(8,128)(2,1)}, bf16[17,16,1024]{2,1,0:T(8,128)(2,1)}) custom-call(s32[1,256]{1,0:T(1,128)} %valid_ref.3, bf16[1,256,1024]{2,1,0:T(8,128)(2,1)} %obs_hbm.3, bf16[1,16,256,1024]{3,2,1,0:T(8,128)(2,1)} %coef_hbm.3), custom_call_target="tpu_custom_call" | custom-call | tf_op jit(solution)/shard_map/rims/pallas_call | solution.py:64
  12.5 0.0 collective-permute-done.1.below_ref
  12.5 0.0 copy-start.3
  12.5 0.0 collective-permute-done.above_ref
  12.6 0.0 copy-start.4
  12.6 0.6 copy-done.3
  13.2 0.0 copy-done.4
  13.2 1.9 %pack.1 = bf16[32,32,384]{2,1,0:T(8,128)(2,1)} custom-call(s32[1,32]{1,0:T(1,128)} %bitcast.10, bf16[4,32,256]{2,1,0:T(8,128)(2,1)} %bitcast.8, bf16[4,32,24]{2,1,0:T(8,128)(2,1)} %copy-done.4, bf16[4,32,24]{2,1,0:T(8,128)(2,1)} %copy-done.3, bf16[17,16,1024]{2,1,0:T(8,128)(2,1)} %get-tuple-element.10.after_ref), custom_call_target="tpu_custom_call" | custom-call | tf_op jit(solution)/shard_map/pack/pallas_call | solution.py:133
  15.1 8.9 %all-to-all-start = ((bf16[32,32,384]{2,1,0:T(8,128)(2,1)}), bf16[32,32,384]{2,1,0:T(8,128)(2,1)S(1)}, u32[]{:S(2)}, u32[]{:S(2)}) async-start(bf16[32,32,384]{2,1,0:T(8,128)(2,1)} %pack.1), calls=%async_computation | async-start | bytes 1572864 | tf_op jit(solution)/shard_map/all_to_all | solution.py:344
  24.0 4.5 %collective-permute-start.2 = (bf16[17,16,1024]{2,1,0:T(8,128)(2,1)}, bf16[17,16,1024]{2,1,0:T(8,128)(2,1)S(1)}, u32[]{:S(2)}, u32[]{:S(2)}) collective-permute-start(bf16[17,16,1024]{2,1,0:T(8,128)(2,1)} %get-tuple-element.15), channel_id=1, source_target_pairs={{0,1},{1,2},{2,3},{4,5},{5,6},{6,7},{8,9},{9,10},{10,11},{12,13},{... | collective-permute-start | bytes 1671176 | tf_op jit(solution)/shard_map/ppermute | solution.py:340
  28.5 1.9 %collective-permute-start.3 = (bf16[17,16,1024]{2,1,0:T(8,128)(2,1)}, bf16[17,16,1024]{2,1,0:T(8,128)(2,1)S(1)}, u32[]{:S(2)}, u32[]{:S(2)}) collective-permute-start(bf16[17,16,1024]{2,1,0:T(8,128)(2,1)} %get-tuple-element.10.after_ref), channel_id=1, source_target_pairs={{1,0},{2,1},{3,2},{5,4},{6,5},{7,6},{9,8},{10,9},{11,10},{13,12},{... | collective-permute-start | bytes 1671176 | tf_op jit(solution)/shard_map/ppermute | solution.py:341
  30.4 4.7 %bands.1 = (bf16[8,256,256]{2,1,0:T(8,128)(2,1)}, bf16[16,144,256]{2,1,0:T(8,128)(2,1)}, bf16[16,128,256]{2,1,0:T(8,128)(2,1)}, bf16[8,768,256]{2,1,0:T(8,128)(2,1)}) custom-call(bf16[16,21]{1,0:T(8,128)(2,1)} %row_ref.1, bf16[16,21]{1,0:T(8,128)(2,1)} %col_ref.1), custom_call_target="tpu_custom_call" | custom-call | tf_op jit(solution)/shard_map/bands/pallas_call | solution.py:109
  35.2 2.2 %collective-permute-done.2.above_hbm = bf16[17,16,1024]{2,1,0:T(8,128)(2,1)S(1)} collective-permute-done((bf16[17,16,1024]{2,1,0:T(8,128)(2,1)}, bf16[17,16,1024]{2,1,0:T(8,128)(2,1)S(1)}, u32[]{:S(2)}, u32[]{:S(2)}) %collective-permute-start.2) | collective-permute-done | bytes 557088 | tf_op jit(solution)/shard_map/ppermute | solution.py:340
  37.4 0.0 copy-start.1
  37.4 3.7 %collective-permute-done.3.below_hbm = bf16[17,16,1024]{2,1,0:T(8,128)(2,1)S(1)} collective-permute-done((bf16[17,16,1024]{2,1,0:T(8,128)(2,1)}, bf16[17,16,1024]{2,1,0:T(8,128)(2,1)S(1)}, u32[]{:S(2)}, u32[]{:S(2)}) %collective-permute-start.3) | collective-permute-done | bytes 557088 | tf_op jit(solution)/shard_map/ppermute | solution.py:341
  41.1 0.0 copy-start.2
  41.1 0.0 all-to-all-done
  41.1 0.0 copy-start
  41.1 0.0 copy-done.1
  41.1 0.9 %copy-done.2 = bf16[17,16,1024]{2,1,0:T(8,128)(2,1)} copy-done((bf16[17,16,1024]{2,1,0:T(8,128)(2,1)}, bf16[17,16,1024]{2,1,0:T(8,128)(2,1)S(1)}, u32[]{:S(2)}) %copy-start.2) | copy-done | bytes 557080
  42.0 0.3 copy-done
  42.2 19.9 %main.1 = (f32[1,256,1024]{2,1,0:T(8,128)}, bf16[1024,256]{1,0:T(8,128)(2,1)}) custom-call(bf16[1024,384]{1,0:T(8,128)(2,1)} %bitcast.5, s32[1,256]{1,0:T(1,128)} %valid_ref.3, bf16[8,256,256]{2,1,0:T(8,128)(2,1)} %get-tuple-element.11.f_hbm, bf16[16,144,256]{2,1,0:T(8,128)(2,1)} %get-tuple-element.12.c_hbm, bf16[16,128,256]{2,1,0:T(8,128)(2,1)} %get-tuple-element.13.a_hbm, ...), custom_call_target="tpu_custom_call" | custom-call | tf_op jit(solution)/shard_map/main/pallas_call | solution.py:281
  62.1 16.4 %all_to_all.10.terms_ref = bf16[32,32,256]{2,1,0:T(8,128)(2,1)} all-to-all(bf16[32,32,256]{2,1,0:T(8,128)(2,1)} %bitcast.6), channel_id=1, replica_groups=mesh['exp'=32,'row'=4] {'exp'}, dimensions={0} | all-to-all | bytes 1048576 | tf_op jit(solution)/shard_map/all_to_all | solution.py:346
  78.5 1.9 %gather.1 = f32[4,32,256]{2,1,0:T(8,128)} custom-call(s32[1,32]{1,0:T(1,128)} %bitcast.11, bf16[32,32,256]{2,1,0:T(8,128)(2,1)} %all_to_all.10.terms_ref), custom_call_target="tpu_custom_call" | custom-call | tf_op jit(solution)/shard_map/gather/pallas_call | solution.py:322
Async XLA Ops:
  1.5 11.0 %collective-permute-start.1 = (bf16[4,32,24]{2,1,0:T(8,128)(2,1)S(1)}, bf16[4,32,24]{2,1,0:T(8,128)(2,1)S(1)}, u32[]{:S(2)}, u32[]{:S(2)}) collective-permute-start(bf16[4,32,24]{2,1,0:T(8,128)(2,1)S(1)} %get-tuple-element.18), channel_id=1, source_target_pairs={{1,0},{2,1},{3,2},{5,4},{6,5},{7,6},{9,8},{10,9},{11,10},{13,12},{... | collective-permute-start | bytes 18440 | tf_op jit(solution)/shard_map/ppermute | solution.py:338
  4.8 7.8 %collective-permute-start = (bf16[4,32,24]{2,1,0:T(8,128)(2,1)S(1)}, bf16[4,32,24]{2,1,0:T(8,128)(2,1)S(1)}, u32[]{:S(2)}, u32[]{:S(2)}) collective-permute-start(bf16[4,32,24]{2,1,0:T(8,128)(2,1)S(1)} %get-tuple-element.19), channel_id=1, source_target_pairs={{0,1},{1,2},{2,3},{4,5},{5,6},{6,7},{8,9},{9,10},{10,11},{12,13},{... | collective-permute-start | bytes 18440 | tf_op jit(solution)/shard_map/ppermute | solution.py:337
  12.5 0.6 copy-start.3
  12.6 0.6 copy-start.4
  15.1 26.0 %all-to-all-start = ((bf16[32,32,384]{2,1,0:T(8,128)(2,1)}), bf16[32,32,384]{2,1,0:T(8,128)(2,1)S(1)}, u32[]{:S(2)}, u32[]{:S(2)}) async-start(bf16[32,32,384]{2,1,0:T(8,128)(2,1)} %pack.1), calls=%async_computation | async-start | bytes 1572864 | tf_op jit(solution)/shard_map/all_to_all | solution.py:344
  24.0 13.4 %collective-permute-start.2 = (bf16[17,16,1024]{2,1,0:T(8,128)(2,1)}, bf16[17,16,1024]{2,1,0:T(8,128)(2,1)S(1)}, u32[]{:S(2)}, u32[]{:S(2)}) collective-permute-start(bf16[17,16,1024]{2,1,0:T(8,128)(2,1)} %get-tuple-element.15), channel_id=1, source_target_pairs={{0,1},{1,2},{2,3},{4,5},{5,6},{6,7},{8,9},{9,10},{10,11},{12,13},{... | collective-permute-start | bytes 1671176 | tf_op jit(solution)/shard_map/ppermute | solution.py:340
  28.5 12.6 %collective-permute-start.3 = (bf16[17,16,1024]{2,1,0:T(8,128)(2,1)}, bf16[17,16,1024]{2,1,0:T(8,128)(2,1)S(1)}, u32[]{:S(2)}, u32[]{:S(2)}) collective-permute-start(bf16[17,16,1024]{2,1,0:T(8,128)(2,1)} %get-tuple-element.10.after_ref), channel_id=1, source_target_pairs={{1,0},{2,1},{3,2},{5,4},{6,5},{7,6},{9,8},{10,9},{11,10},{13,12},{... | collective-permute-start | bytes 1671176 | tf_op jit(solution)/shard_map/ppermute | solution.py:341
  37.4 3.7 %copy-start.1 = (bf16[17,16,1024]{2,1,0:T(8,128)(2,1)}, bf16[17,16,1024]{2,1,0:T(8,128)(2,1)S(1)}, u32[]{:S(2)}) copy-start(bf16[17,16,1024]{2,1,0:T(8,128)(2,1)S(1)} %collective-permute-done.2.above_hbm) | copy-start | bytes 1671172
  41.1 0.9 %copy-start.2 = (bf16[17,16,1024]{2,1,0:T(8,128)(2,1)}, bf16[17,16,1024]{2,1,0:T(8,128)(2,1)S(1)}, u32[]{:S(2)}) copy-start(bf16[17,16,1024]{2,1,0:T(8,128)(2,1)S(1)} %collective-permute-done.3.below_hbm) | copy-start | bytes 1671172
  41.1 1.1 %copy-start = (bf16[32,32,384]{2,1,0:T(8,128)(2,1)}, bf16[32,32,384]{2,1,0:T(8,128)(2,1)S(1)}, u32[]{:S(2)}) copy-start(bf16[32,32,384]{2,1,0:T(8,128)(2,1)S(1)} %all-to-all-done) | copy-start | bytes 2359300

commit v3 on v2

--- a/solution.py
+++ b/solution.py
@@ -4,6 +4,7 @@
 from jax.experimental import pallas as pl
 from jax.experimental.pallas import tpu as pltpu
 from jax.sharding import PartitionSpec as P
+
 
 F32 = jnp.float32
 BF16 = jnp.bfloat16
@@ -40,35 +41,65 @@
     return jnp.broadcast_to(valid, (128, valid.shape[1])).T
 
 
-def rims_kernel(valid_ref, obs_hbm, coef_hbm, up_ref, down_ref, head, tail, sem):
+def stage_kernel(
+    cell_ref, lat_ref, above_ref, below_ref, valid_ref, obs_hbm, coef_hbm,
+    packed_hbm, up_hbm, down_hbm,
+    turned, packed, head, tail, sem, out_sem,
+):
+    last = pl.ds(ROWS - RIM, RIM)
     copies = [
         pltpu.make_async_copy(coef_hbm.at[0, :, pl.ds(0, RIM), :], head.at[pl.ds(0, KERNELS)], sem.at[0]),
-        pltpu.make_async_copy(coef_hbm.at[0, :, pl.ds(ROWS - RIM, RIM), :], tail.at[pl.ds(0, KERNELS)], sem.at[1]),
+        pltpu.make_async_copy(coef_hbm.at[0, :, last, :], tail.at[pl.ds(0, KERNELS)], sem.at[1]),
         pltpu.make_async_copy(obs_hbm.at[0, pl.ds(0, RIM), :], head.at[KERNELS], sem.at[2]),
-        pltpu.make_async_copy(obs_hbm.at[0, pl.ds(ROWS - RIM, RIM), :], tail.at[KERNELS], sem.at[3]),
+        pltpu.make_async_copy(obs_hbm.at[0, last, :], tail.at[KERNELS], sem.at[3]),
+    ]
+    outs = [
+        pltpu.make_async_copy(packed, packed_hbm, out_sem.at[0]),
+        pltpu.make_async_copy(head, up_hbm, out_sem.at[1]),
+        pltpu.make_async_copy(tail, down_hbm, out_sem.at[2]),
     ]
     for copy in copies:
         copy.start()
+    fill = jnp.zeros((OWN, LATP - LAT), BF16)
+    for c in range(CELLS):
+        parts = [above_ref[c][:, ROWS - SKY :], lat_ref[c], below_ref[c][:, :SKY], fill]
+        turned[c] = jnp.concatenate(parts, axis=1)
+    for e in range(EXPOSURES):
+        packed[e] = turned[cell_ref[0, e]]
+    outs[0].start()
     mask = column_of(valid_ref[...].astype(F32))
     head_mask = jnp.concatenate([mask[:RIM]] * BLOCKS, axis=1)
     tail_mask = jnp.concatenate([mask[ROWS - RIM :]] * BLOCKS, axis=1)
     for copy in copies:
         copy.wait()
     for k in range(KERNELS + 1):
-        up_ref[k] = (head[k].astype(F32) * head_mask).astype(BF16)
-        down_ref[k] = (tail[k].astype(F32) * tail_mask).astype(BF16)
-
-
-def rims(valid, observed, coefficients):
+        head[k] = (head[k].astype(F32) * head_mask).astype(BF16)
+    outs[1].start()
+    for k in range(KERNELS + 1):
+        tail[k] = (tail[k].astype(F32) * tail_mask).astype(BF16)
+    outs[2].start()
+    for copy in outs:
+        copy.wait()
+
+
+def stage(cell_of, latent, above, below, valid, observed, coefficients):
     rim = (KERNELS + 1, RIM, COLS)
+    packed = (EXPOSURES, OWN, LATP)
     return pl.pallas_call(
-        rims_kernel,
-        out_shape=(jax.ShapeDtypeStruct(rim, BF16),) * 2,
-        in_specs=[VMEM, ANY, ANY],
-        out_specs=(VMEM,) * 2,
-        scratch_shapes=[pltpu.VMEM(rim, BF16), pltpu.VMEM(rim, BF16), pltpu.SemaphoreType.DMA((4,))],
-        name="rims",
-    )(valid, observed, coefficients)
+        stage_kernel,
+        out_shape=(jax.ShapeDtypeStruct(packed, BF16),) + (jax.ShapeDtypeStruct(rim, BF16),) * 2,
+        in_specs=[SMEM, VMEM, VMEM, VMEM, VMEM, ANY, ANY],
+        out_specs=(ANY,) * 3,
+        scratch_shapes=[
+            pltpu.VMEM((CELLS, OWN, LATP), BF16),
+            pltpu.VMEM(packed, BF16),
+            pltpu.VMEM(rim, BF16),
+            pltpu.VMEM(rim, BF16),
+            pltpu.SemaphoreType.DMA((4,)),
+            pltpu.SemaphoreType.DMA((3,)),
+        ],
+        name="stage",
+    )(cell_of, latent, above, below, valid, observed, coefficients)
 
 
 def base_rows(taps, place):
@@ -118,26 +149,6 @@
         out_specs=(VMEM,) * 4,
         name="bands",
     )(row_taps, column_taps)
-
-
-def pack_kernel(cell_ref, lat_ref, above_ref, below_ref, after_ref, out_ref, turned):
-    for c in range(CELLS):
-        turned[c] = jnp.concatenate(
-            [above_ref[c], lat_ref[c], below_ref[c], jnp.zeros((OWN, LATP - LAT), BF16)], axis=1
-        )
-    for e in range(EXPOSURES):
-        out_ref[e] = turned[cell_ref[0, e]]
-
-
-def pack(cell_of, latent, above, below, after):
-    return pl.pallas_call(
-        pack_kernel,
-        out_shape=jax.ShapeDtypeStruct((EXPOSURES, OWN, LATP), BF16),
-        in_specs=[SMEM, VMEM, VMEM, VMEM, ANY],
-        out_specs=VMEM,
-        scratch_shapes=[pltpu.VMEM((CELLS, OWN, LATP), BF16)],
-        name="pack",
-    )(cell_of, latent, above, below, after)
 
 
 def main_kernel(
@@ -334,14 +345,14 @@
     upward = [(i + 1, i) for i in range(count - 1)]
     cell_of = cell_of.reshape(1, EXPOSURES)
     latent = jnp.swapaxes(latent, 1, 2)
-    sky_above = lax.ppermute(latent[:, :, ROWS - SKY :], "row", downward)
-    sky_below = lax.ppermute(latent[:, :, :SKY], "row", upward)
-    head, tail = rims(valid_rows, observed, coefficients)
+    sky_above = lax.ppermute(latent, "row", downward)
+    sky_below = lax.ppermute(latent, "row", upward)
+    packed, head, tail = stage(cell_of, latent, sky_above, sky_below, valid_rows, observed, coefficients)
     above = lax.ppermute(tail, "row", downward)
     below = lax.ppermute(head, "row", upward)
-    packed = pack(cell_of, latent, sky_above, sky_below, head)
+    strip = lax.all_to_all(packed, "exp", 0, 0, tiled=True)
     bands = make_bands(row_taps, column_taps)
-    strip = lax.all_to_all(packed, "exp", 0, 0, tiled=True).reshape(COLS, LATP)
+    strip = strip.reshape(COLS, LATP)
     residual, send = main(strip, valid_rows, bands, coefficients, observed, above, below)
     terms = lax.all_to_all(send.reshape(EXPOSURES, OWN, ROWS), "exp", 0, 0, tiled=True)
     return jnp.swapaxes(gather(cell_of, terms), 1, 2), residual

time: 81 us -> 82.3 us (1.016)
  starting transfers between devices: 23.3 us -> 25.3 us
  waiting for transfers between devices: 5.93 us -> 7.55 us
  Pallas kernels: 31.5 us -> 30.1 us
  local copies, waits for them, and re-layouts: 2.58 us -> 1.73 us
    ppermute x1, waiting for transfers between devices: 2.23 us -> 0.13 us  [body(): above = lax.ppermute(tail, 'row', downward)]
    ppermute x1, waiting for transfers between devices: 3.7 us -> 5.79 us  [body(): below = lax.ppermute(head, 'row', upward)]
    ppermute x1, starting transfers between devices: 4.5 us -> 6.55 us  [body(): above = lax.ppermute(tail, 'row', downward)]
    ppermute x2, waiting for transfers between devices: 0.01 us -> 1.62 us  [the longest x1 1.41 us: body(): sky_above = lax.ppermute(latent, 'row', downward)]
    pallas_call x2 -> x1, Pallas kernels: 4.99 us -> 3.56 us  [stage(): pl.pallas_call(stage_kernel, out_shape=(jax.ShapeDtypeStruct(packed, BF16...]
    slice x1 -> x0, local copies, waits for them, and re-layouts: 0.85 us -> none  [body(): sky_below = lax.ppermute(latent[:, :, :SKY], 'row', upward)]
  transfers between devices with their start and end apart: 5 -> 5, of which waited for: 2 -> 4; matrix products, arithmetic and copies ran while one was open for 0% -> 0% of each run, Pallas kernels for 10% -> 6%
where the time goes in v3:
time: 82.3 us; the launch traced here: 81.8 us
  Pallas kernels  30.1 us (37%)
  starting transfers between devices  25.3 us (31%)
  blocking collectives  16.4 us (20%)
  waiting for transfers between devices  7.55 us (9%)
  local copies, waits for them, and re-layouts  1.73 us (2%)
    pallas_call x1, Pallas kernels, main(): pl.pallas_call(main_kernel, out_shape=(jax.ShapeDtypeStruct((1, ROWS, COL...  19.9 us
    all_to_all x1, blocking collectives, body(): lax.all_to_all(send.reshape(EXPOSURES, OWN, ROWS), 'exp', 0, 0, tiled=True)  16.4 us
    all_to_all x1, starting transfers between devices, body(): strip = lax.all_to_all(packed, 'exp', 0, 0, tiled=True)  8.93 us
    ppermute x1, starting transfers between devices, body(): above = lax.ppermute(tail, 'row', downward)  6.55 us
    ppermute x1, waiting for transfers between devices, body(): below = lax.ppermute(head, 'row', upward)  5.79 us
    pallas_call x1, Pallas kernels, make_bands(): pl.pallas_call(bands_kernel, out_shape=(jax.ShapeDtypeStruct((PAIRS, 256,...  4.71 us
    ppermute x1, starting transfers between devices, body(): sky_above = lax.ppermute(latent, 'row', downward)  4.66 us
    pallas_call x1, Pallas kernels, stage(): pl.pallas_call(stage_kernel, out_shape=(jax.ShapeDtypeStruct(packed, BF16...  3.56 us
  transfers between devices with their start and end apart: 5, of which 4 were waited for; matrix products, arithmetic and copies ran while one was open for 0% of the time, Pallas kernels for 6%

profile of v3, /device:TPU:1, one launch (start us, length us, event | category | flops | bytes accessed | tf_op | source)
XLA Modules:
  0.0 81.8 jit_solution(13006328214440397275)
XLA Ops:
  0.6 3.3 %collective-permute-start.1 = (bf16[4,32,256]{2,1,0:T(8,128)(2,1)}, bf16[4,32,256]{2,1,0:T(8,128)(2,1)S(1)}, u32[]{:S(2)}, u32[]{:S(2)}) collective-permute-start(bf16[4,32,256]{2,1,0:T(8,128)(2,1)} %bitcast.8), channel_id=1, source_target_pairs={{1,0},{2,1},{3,2},{5,4},{6,5},{7,6},{9,8},{10,9},{11,10},{13,12},{... | collective-permute-start | bytes 196616 | tf_op jit(solution)/shard_map/ppermute | solution.py:349
  3.9 4.7 %collective-permute-start = (bf16[4,32,256]{2,1,0:T(8,128)(2,1)}, bf16[4,32,256]{2,1,0:T(8,128)(2,1)S(1)}, u32[]{:S(2)}, u32[]{:S(2)}) collective-permute-start(bf16[4,32,256]{2,1,0:T(8,128)(2,1)} %bitcast.9), channel_id=1, source_target_pairs={{0,1},{1,2},{2,3},{4,5},{5,6},{6,7},{8,9},{9,10},{10,11},{12,13},{... | collective-permute-start | bytes 196616 | tf_op jit(solution)/shard_map/ppermute | solution.py:348
  8.6 0.2 collective-permute-done.1.below_ref
  8.8 0.0 copy-start.3
  8.8 1.4 %collective-permute-done.above_ref = bf16[4,32,256]{2,1,0:T(8,128)(2,1)S(1)} collective-permute-done((bf16[4,32,256]{2,1,0:T(8,128)(2,1)}, bf16[4,32,256]{2,1,0:T(8,128)(2,1)S(1)}, u32[]{:S(2)}, u32[]{:S(2)}) %collective-permute-start) | collective-permute-done | bytes 65568 | tf_op jit(solution)/shard_map/ppermute | solution.py:348
  10.2 0.0 copy-start.4
  10.2 0.0 copy-done.3
  10.2 0.6 copy-done.4
  10.8 3.6 %stage.1 = (bf16[32,32,384]{2,1,0:T(8,128)(2,1)}, bf16[17,16,1024]{2,1,0:T(8,128)(2,1)}, bf16[17,16,1024]{2,1,0:T(8,128)(2,1)}) custom-call(s32[1,32]{1,0:T(1,128)} %bitcast.11, bf16[4,32,256]{2,1,0:T(8,128)(2,1)} %bitcast.10, bf16[4,32,256]{2,1,0:T(8,128)(2,1)} %copy-done.4, bf16[4,32,256]{2,1,0:T(8,128)(2,1)} %copy-done.3, s32[1,256]{1,0:T(1,128)} %valid_ref.3, ...), custom_call_target="tpu_custom_call" | custom-call | tf_op jit(solution)/shard_map/stage/pallas_call | solution.py:88
  14.4 8.9 %all-to-all-start = ((bf16[32,32,384]{2,1,0:T(8,128)(2,1)}), bf16[32,32,384]{2,1,0:T(8,128)(2,1)S(1)}, u32[]{:S(2)}, u32[]{:S(2)}) async-start(bf16[32,32,384]{2,1,0:T(8,128)(2,1)} %get-tuple-element.11), calls=%async_computation | async-start | bytes 1572864 | tf_op jit(solution)/shard_map/all_to_all | solution.py:353
  23.4 6.6 %collective-permute-start.2 = (bf16[17,16,1024]{2,1,0:T(8,128)(2,1)}, bf16[17,16,1024]{2,1,0:T(8,128)(2,1)S(1)}, u32[]{:S(2)}, u32[]{:S(2)}) collective-permute-start(bf16[17,16,1024]{2,1,0:T(8,128)(2,1)} %get-tuple-element.16), channel_id=1, source_target_pairs={{0,1},{1,2},{2,3},{4,5},{5,6},{6,7},{8,9},{9,10},{10,11},{12,13},{... | collective-permute-start | bytes 1671176 | tf_op jit(solution)/shard_map/ppermute | solution.py:351
  29.9 1.9 %collective-permute-start.3 = (bf16[17,16,1024]{2,1,0:T(8,128)(2,1)}, bf16[17,16,1024]{2,1,0:T(8,128)(2,1)S(1)}, u32[]{:S(2)}, u32[]{:S(2)}) collective-permute-start(bf16[17,16,1024]{2,1,0:T(8,128)(2,1)} %get-tuple-element.17), channel_id=1, source_target_pairs={{1,0},{2,1},{3,2},{5,4},{6,5},{7,6},{9,8},{10,9},{11,10},{13,12},{... | collective-permute-start | bytes 1671176 | tf_op jit(solution)/shard_map/ppermute | solution.py:352
  31.8 4.7 %bands.1 = (bf16[8,256,256]{2,1,0:T(8,128)(2,1)}, bf16[16,144,256]{2,1,0:T(8,128)(2,1)}, bf16[16,128,256]{2,1,0:T(8,128)(2,1)}, bf16[8,768,256]{2,1,0:T(8,128)(2,1)}) custom-call(bf16[16,21]{1,0:T(8,128)(2,1)} %row_ref.1, bf16[16,21]{1,0:T(8,128)(2,1)} %col_ref.1), custom_call_target="tpu_custom_call" | custom-call | tf_op jit(solution)/shard_map/bands/pallas_call | solution.py:140
  36.6 0.1 collective-permute-done.2.above_hbm
  36.7 0.0 copy-start.1
  36.7 5.8 %collective-permute-done.3.below_hbm = bf16[17,16,1024]{2,1,0:T(8,128)(2,1)S(1)} collective-permute-done((bf16[17,16,1024]{2,1,0:T(8,128)(2,1)}, bf16[17,16,1024]{2,1,0:T(8,128)(2,1)S(1)}, u32[]{:S(2)}, u32[]{:S(2)}) %collective-permute-start.3) | collective-permute-done | bytes 557088 | tf_op jit(solution)/shard_map/ppermute | solution.py:352
  42.5 0.0 copy-start.2
  42.5 0.0 all-to-all-done
  42.5 0.0 copy-start
  42.5 0.0 copy-done.1
  42.5 0.8 %copy-done.2 = bf16[17,16,1024]{2,1,0:T(8,128)(2,1)} copy-done((bf16[17,16,1024]{2,1,0:T(8,128)(2,1)}, bf16[17,16,1024]{2,1,0:T(8,128)(2,1)S(1)}, u32[]{:S(2)}) %copy-start.2) | copy-done | bytes 557080
  43.3 0.3 copy-done
  43.6 19.9 %main.1 = (f32[1,256,1024]{2,1,0:T(8,128)}, bf16[1024,256]{1,0:T(8,128)(2,1)}) custom-call(bf16[1024,384]{1,0:T(8,128)(2,1)} %bitcast.5, s32[1,256]{1,0:T(1,128)} %valid_ref.3, bf16[8,256,256]{2,1,0:T(8,128)(2,1)} %get-tuple-element.12.f_hbm, bf16[16,144,256]{2,1,0:T(8,128)(2,1)} %get-tuple-element.13.c_hbm, bf16[16,128,256]{2,1,0:T(8,128)(2,1)} %get-tuple-element.14.a_hbm, ...), custom_call_target="tpu_custom_call" | custom-call | tf_op jit(solution)/shard_map/main/pallas_call | solution.py:292
  63.5 16.4 %all_to_all.10.terms_ref = bf16[32,32,256]{2,1,0:T(8,128)(2,1)} all-to-all(bf16[32,32,256]{2,1,0:T(8,128)(2,1)} %bitcast.6), channel_id=1, replica_groups=mesh['exp'=32,'row'=4] {'exp'}, dimensions={0} | all-to-all | bytes 1048576 | tf_op jit(solution)/shard_map/all_to_all | solution.py:357
  79.9 1.9 %gather.1 = f32[4,32,256]{2,1,0:T(8,128)} custom-call(s32[1,32]{1,0:T(1,128)} %bitcast.12, bf16[32,32,256]{2,1,0:T(8,128)(2,1)} %all_to_all.10.terms_ref), custom_call_target="tpu_custom_call" | custom-call | tf_op jit(solution)/shard_map/gather/pallas_call | solution.py:333
Async XLA Ops:
  0.6 8.2 %collective-permute-start.1 = (bf16[4,32,256]{2,1,0:T(8,128)(2,1)}, bf16[4,32,256]{2,1,0:T(8,128)(2,1)S(1)}, u32[]{:S(2)}, u32[]{:S(2)}) collective-permute-start(bf16[4,32,256]{2,1,0:T(8,128)(2,1)} %bitcast.8), channel_id=1, source_target_pairs={{1,0},{2,1},{3,2},{5,4},{6,5},{7,6},{9,8},{10,9},{11,10},{13,12},{... | collective-permute-start | bytes 196616 | tf_op jit(solution)/shard_map/ppermute | solution.py:349
  3.9 6.3 %collective-permute-start = (bf16[4,32,256]{2,1,0:T(8,128)(2,1)}, bf16[4,32,256]{2,1,0:T(8,128)(2,1)S(1)}, u32[]{:S(2)}, u32[]{:S(2)}) collective-permute-start(bf16[4,32,256]{2,1,0:T(8,128)(2,1)} %bitcast.9), channel_id=1, source_target_pairs={{0,1},{1,2},{2,3},{4,5},{5,6},{6,7},{8,9},{9,10},{10,11},{12,13},{... | collective-permute-start | bytes 196616 | tf_op jit(solution)/shard_map/ppermute | solution.py:348
  8.8 1.4 %copy-start.3 = (bf16[4,32,256]{2,1,0:T(8,128)(2,1)}, bf16[4,32,256]{2,1,0:T(8,128)(2,1)S(1)}, u32[]{:S(2)}) copy-start(bf16[4,32,256]{2,1,0:T(8,128)(2,1)S(1)} %collective-permute-done.1.below_ref) | copy-start | bytes 196612
  10.2 0.6 copy-start.4
  14.4 28.1 %all-to-all-start = ((bf16[32,32,384]{2,1,0:T(8,128)(2,1)}), bf16[32,32,384]{2,1,0:T(8,128)(2,1)S(1)}, u32[]{:S(2)}, u32[]{:S(2)}) async-start(bf16[32,32,384]{2,1,0:T(8,128)(2,1)} %get-tuple-element.11), calls=%async_computation | async-start | bytes 1572864 | tf_op jit(solution)/shard_map/all_to_all | solution.py:353
  23.4 13.3 %collective-permute-start.2 = (bf16[17,16,1024]{2,1,0:T(8,128)(2,1)}, bf16[17,16,1024]{2,1,0:T(8,128)(2,1)S(1)}, u32[]{:S(2)}, u32[]{:S(2)}) collective-permute-start(bf16[17,16,1024]{2,1,0:T(8,128)(2,1)} %get-tuple-element.16), channel_id=1, source_target_pairs={{0,1},{1,2},{2,3},{4,5},{5,6},{6,7},{8,9},{9,10},{10,11},{12,13},{... | collective-permute-start | bytes 1671176 | tf_op jit(solution)/shard_map/ppermute | solution.py:351
  29.9 12.6 %collective-permute-start.3 = (bf16[17,16,1024]{2,1,0:T(8,128)(2,1)}, bf16[17,16,1024]{2,1,0:T(8,128)(2,1)S(1)}, u32[]{:S(2)}, u32[]{:S(2)}) collective-permute-start(bf16[17,16,1024]{2,1,0:T(8,128)(2,1)} %get-tuple-element.17), channel_id=1, source_target_pairs={{1,0},{2,1},{3,2},{5,4},{6,5},{7,6},{9,8},{10,9},{11,10},{13,12},{... | collective-permute-start | bytes 1671176 | tf_op jit(solution)/shard_map/ppermute | solution.py:352
  36.7 5.8 %copy-start.1 = (bf16[17,16,1024]{2,1,0:T(8,128)(2,1)}, bf16[17,16,1024]{2,1,0:T(8,128)(2,1)S(1)}, u32[]{:S(2)}) copy-start(bf16[17,16,1024]{2,1,0:T(8,128)(2,1)S(1)} %collective-permute-done.2.above_hbm) | copy-start | bytes 1671172
  42.5 0.9 %copy-start.2 = (bf16[17,16,1024]{2,1,0:T(8,128)(2,1)}, bf16[17,16,1024]{2,1,0:T(8,128)(2,1)S(1)}, u32[]{:S(2)}) copy-start(bf16[17,16,1024]{2,1,0:T(8,128)(2,1)S(1)} %collective-permute-done.3.below_hbm) | copy-start | bytes 1671172
  42.5 1.1 %copy-start = (bf16[32,32,384]{2,1,0:T(8,128)(2,1)}, bf16[32,32,384]{2,1,0:T(8,128)(2,1)S(1)}, u32[]{:S(2)}) copy-start(bf16[32,32,384]{2,1,0:T(8,128)(2,1)S(1)} %all-to-all-done) | copy-start | bytes 2359300
